TPU v7x, 256 devices: a whole 4x4x8 slice. The times are simulated.
256 devices in a mesh: row: 32 (over z, y), col: 8 (over x, core).
Axes of the slice: x: 4, y: 4, z: 8, core: 2. Of those that a mesh axis runs over, the one named last changes fastest.
Arguments:
- obstacles: float32 [3, 16384], P(None, 'row'), may hold values from 0 to 16
- particles: float32 [3, 8192], P(None, 'row'), may hold values from 0 to 16
- forces: float32 [3, 32, 8192], P(None, None, 'row'), may hold values from -0.8 to 0.8
- neighbours: int32 [64, 32], P('row', 'col'), may hold values from 0 to 127, as said below
- carried: float32 [128, 3, 32, 128], P('row'), may hold values from -6 to 6
- factor: float32 [2, 4096, 128, 3, 128], P(None, 'col', 'row'), may hold values from -0.09375 to 0.09375
- inverses: float32 [2, 4096, 4096], P(None, 'row', 'col'), may hold values from -0.09375 to 0.09375
Outputs:
- solved: float32 [2, 32, 4096], P(None, None, 'col')
- remaining: float32 [128, 3, 32, 128], P('row', None, 'col')
Inputs may be any that keep to these rules, and one draw needn't show every extreme that they name: `neighbours`: each particle block lists 32 different obstacle blocks, and every obstacle block is listed by exactly 16 particle blocks.
All inputs are finite; a program needn't handle non-finite values.
Results may differ from a plain program's by a relative error of at most 0.0001.
Values sent between devices are 32-bit elements; how exact they have to be, the bound alone decides.
No kernel may reach another device: no remote copies, remote signals or barrier semaphores. Data moves between devices by JAX's collectives and lax.ppermute only.
A program may use at most 64 MiB of HBM per device.

v0:
```python
import functools

import jax
import jax.numpy as jnp
from jax import lax
from jax.experimental import pallas as pl
from jax.experimental.pallas import tpu as pltpu
from jax.sharding import PartitionSpec as P

ROWS = 32
COLS = 8
BLOCKS_DEV = 4
SLICE = 32
RHS = 32
COMPS = 3
PAIRS = ((0, 0), (1, 1), (2, 2), (0, 1), (0, 2), (1, 2))
SHARE = RHS // COLS
COLUMNS = 512

ON_CHIP = pl.BlockSpec(memory_space=pltpu.VMEM)
IN_PLACE = pl.BlockSpec(memory_space=pltpu.HBM)
GRANT = pltpu.CompilerParams(vmem_limit_bytes=16 << 20)


def kept(shape, dtype=jnp.float32):
    return pltpu.VMEM(shape, dtype)


def keep(array):
    return pltpu.with_memory_space_constraint(array, pltpu.VMEM)


def stay(array):
    return pltpu.with_memory_space_constraint(array, pltpu.HBM)


def halves(value):
    high = value.astype(jnp.bfloat16)
    return high, (value - high.astype(jnp.float32)).astype(jnp.bfloat16)


def product(left, high, low):
    top, rest = halves(left)
    both = jnp.concatenate([top, rest], axis=0)
    full = jnp.dot(both, high, preferred_element_type=jnp.float32)
    part = jnp.dot(top, low, preferred_element_type=jnp.float32)
    count = left.shape[0]
    return full[:count] + full[count:] + part


def payload_kernel(
    forces_hbm, particles_hbm, neighbours_hbm, out_hbm, forces_ref, particles_ref, neighbours_ref, sent, read, wrote
):
    col = lax.axis_index("col")
    start = pl.multiple_of((col // 2) * 8, 8)
    copies = [
        pltpu.make_async_copy(forces_hbm.at[:, pl.ds(start, 8), :], forces_ref, read.at[0]),
        pltpu.make_async_copy(particles_hbm, particles_ref, read.at[1]),
        pltpu.make_async_copy(neighbours_hbm, neighbours_ref, read.at[2]),
    ]
    for copy in copies:
        copy.start()
    lane = lax.broadcasted_iota(jnp.int32, (8, 128), 1)
    line = lax.broadcasted_iota(jnp.int32, (8, 128), 0)
    odd = jnp.full((8, 128), col % 2, jnp.int32) == 1
    for copy in copies:
        copy.wait()
    for half in range(2):
        sides = []
        for comp in range(COMPS):
            eight = forces_ref[comp, :, pl.ds(128 * half, 128)]
            sides.append(jnp.where(odd, pltpu.roll(eight, 4, axis=0), eight))
        place = jnp.concatenate(
            [particles_ref[:, pl.ds(128 * half, 128)], jnp.zeros((5, 128), jnp.float32)], axis=0
        )
        listed = jnp.full((8, 128), -1.0, jnp.float32)
        for entry in range(4):
            name = jnp.full((8, 128), neighbours_ref[half, entry], jnp.int32).astype(jnp.float32)
            listed = jnp.where(lane == 96 + entry, name, listed)
        for quarter in range(4):
            value = None
            for at, piece in enumerate([*sides, place]):
                turn = (SLICE * (at - quarter)) % 128
                piece = pltpu.roll(piece, turn, axis=1) if turn else piece
                value = piece if value is None else jnp.where(lane >= SLICE * at, piece, value)
            value = jnp.where((lane >= 96) & (line == 3), listed, value)
            sent[4 * half + quarter] = value[0:4]
    copies = [pltpu.make_async_copy(sent, out_hbm.at[row], wrote.at[row]) for row in range(ROWS)]
    for copy in copies:
        copy.start()
    for copy in copies:
        copy.wait()


def payload(forces, particles, neighbours):
    return pl.pallas_call(
        payload_kernel,
        out_shape=pltpu.HBM((ROWS, COLS, SHARE, 128), jnp.float32),
        in_specs=[IN_PLACE] * 3,
        out_specs=IN_PLACE,
        scratch_shapes=[
            pltpu.VMEM((COMPS, 8, 256), jnp.float32),
            pltpu.VMEM((COMPS, 256), jnp.float32),
            pltpu.SMEM((2, 4), jnp.int32),
            pltpu.VMEM((COLS, SHARE, 128), jnp.float32),
            pltpu.SemaphoreType.DMA((3,)),
            pltpu.SemaphoreType.DMA((ROWS,)),
        ],
        name="payload",
        compiler_params=GRANT,
    )(stay(forces), stay(particles), stay(neighbours))


def prepare_kernel(
    factor_ref, inverses_ref, carried_ref, fh_ref, fl_ref, dh_ref, dl_ref, ih_ref, il_ref, mine_ref
):
    for panel in range(2):
        for comp in range(COMPS):
            for block in range(BLOCKS_DEV):
                rows = pl.ds(BLOCKS_DEV * comp + block, COLUMNS, stride=COMPS * BLOCKS_DEV)
                high, low = halves(factor_ref[panel, rows, :])
                pair = 2 * comp + block // 2
                lanes = pl.ds(128 * (block % 2), 128)
                fh_ref[panel, pair, :, lanes] = high
                fl_ref[panel, pair, :, lanes] = low
                if panel == 0 and comp == 1 and block == 0:
                    dh_ref[...] = high
                    dl_ref[...] = low
        high, low = halves(inverses_ref[panel])
        ih_ref[panel] = high
        il_ref[panel] = low
    owner = lax.broadcasted_iota(jnp.int32, (RHS, 128), 0) // SHARE
    own = owner == jnp.full((RHS, 128), lax.axis_index("col"), jnp.int32)
    for block in range(BLOCKS_DEV):
        for comp in range(COMPS):
            mine_ref[block, comp] = jnp.where(own, carried_ref[block, comp], 0.0)


def prepare(factor_rows, inverses, carried):
    panels = (2, 2 * COMPS, COLUMNS, 256)
    return pl.pallas_call(
        prepare_kernel,
        out_shape=(
            pltpu.HBM(panels, jnp.bfloat16),
            pltpu.HBM(panels, jnp.bfloat16),
            kept((COLUMNS, 128), jnp.bfloat16),
            kept((COLUMNS, 128), jnp.bfloat16),
            kept(inverses.shape, jnp.bfloat16),
            kept(inverses.shape, jnp.bfloat16),
            kept(carried.shape),
        ),
        in_specs=[ON_CHIP] * 3,
        out_specs=(ON_CHIP,) * 7,
        name="prepare",
        compiler_params=GRANT,
    )(factor_rows, inverses, carried)


def couple(blocks, points_ref, flags_ref, push_ref, source_ref, high, low):
    width = 128 * len(blocks)
    totals = [None] * COMPS
    for tile in range(4):
        slot = tile % 2
        for where, block in enumerate(blocks):
            lanes = pl.ds(128 * where, 128)
            points = [points_ref[c : c + 1, pl.ds(128 * block, 128)] for c in range(COMPS)]
            flags = flags_ref[block : block + 1, :]
            for at in range(8):
                group = 8 * tile + at
                rows = pl.ds(SLICE * at, SLICE)
                spots = pl.ds(SLICE * group, SLICE)
                diff = [points[c] - source_ref[c, spots, :] for c in range(COMPS)]
                flag = jnp.broadcast_to(flags[:, 8 * group : 8 * group + 1], (SLICE, 128))
                radius = diff[0] * diff[0] + diff[1] * diff[1] + diff[2] * diff[2] + 1.0
                root = lax.rsqrt(radius)
                cube = root * root * root * flag
                iso = (radius + 1.0) * cube
                scaled = [diff[0] * cube, diff[1] * cube, diff[2] * cube]
                for n, (a, b) in enumerate(PAIRS):
                    value = scaled[a] * diff[b]
                    top, rest = halves(value + iso if a == b else value)
                    high[slot, n, rows, lanes] = top
                    low[slot, n, rows, lanes] = rest
        for n, (a, b) in enumerate(PAIRS):
            if a == b:
                left, first = push_ref[b, tile], push_ref[b, tile, 0:32]
            else:
                left = jnp.concatenate([push_ref[b, tile], push_ref[a, tile]], axis=0)
                first = jnp.concatenate(
                    [push_ref[b, tile, 0:32], push_ref[a, tile, 0:32]], axis=0
                )
            full = jnp.dot(left, high[slot, n, :, 0:width], preferred_element_type=jnp.float32)
            rest = jnp.dot(first, low[slot, n, :, 0:width], preferred_element_type=jnp.float32)
            add = full[0:32] + full[32:64] + rest[0:32]
            totals[a] = add if totals[a] is None else totals[a] + add
            if a != b:
                add = full[64:96] + full[96:128] + rest[32:64]
                totals[b] = add if totals[b] is None else totals[b] + add
    return totals


def near_first_kernel(
    got_ref, points_ref, mine_ref, out_ref, spread_ref, push_ref, source_ref, flags_ref, high, low
):
    lane = lax.broadcasted_iota(jnp.int32, (RHS, 128), 1) // SLICE
    for quad in range(8):
        for comp in range(COMPS):
            joined = None
            for at in range(4):
                piece = got_ref[pl.ds(RHS * (4 * quad + at), RHS), :]
                turn = (SLICE * (at - comp)) % 128
                piece = pltpu.roll(piece, turn, axis=1) if turn else piece
                joined = piece if joined is None else jnp.where(lane == at, piece, joined)
            top, rest = halves(joined)
            lanes = pl.ds(128 * (quad % 2), 128)
            push_ref[comp, quad // 2, 0:32, lanes] = top
            push_ref[comp, quad // 2, 32:64, lanes] = rest
    for comp in range(COMPS):
        places = got_ref[pl.ds(comp, ROWS, stride=RHS), :].T
        for group in range(ROWS):
            column = places[96:128, group : group + 1]
            source_ref[comp, pl.ds(SLICE * group, SLICE), :] = jnp.broadcast_to(column, (SLICE, 128))
    lists = got_ref[pl.ds(3, ROWS * COLS, stride=4), :].T[96:104, :]
    first = BLOCKS_DEV * lax.axis_index("row")
    for block in range(BLOCKS_DEV):
        name = jnp.full(lists.shape, first + block, jnp.int32).astype(jnp.float32)
        found = jnp.where(lists == name, 1.0, 0.0)
        for step in (1, 2, 4):
            found = jnp.maximum(found, pltpu.roll(found, ROWS * COLS - step, axis=1))
        flags_ref[block : block + 1, :] = jnp.max(found, axis=0, keepdims=True)
    totals = couple((0,), points_ref, flags_ref, push_ref, source_ref, high, low)
    for comp in range(COMPS):
        value = totals[comp] + mine_ref[0, comp]
        out_ref[comp] = value
        if comp == 0:
            for part in range(COLS):
                spread_ref[part] = value


def near_first(got, points, mine):
    return pl.pallas_call(
        near_first_kernel,
        out_shape=(
            kept((COMPS, RHS, 128)),
            kept((COLS, RHS, 128)),
            kept((COMPS, 4, 64, 256), jnp.bfloat16),
            kept((COMPS, ROWS * SLICE, 128)),
            kept((BLOCKS_DEV, 256)),
        ),
        in_specs=[ON_CHIP] * 3,
        out_specs=(ON_CHIP,) * 5,
        scratch_shapes=[pltpu.VMEM((2, 6, 256, 128), jnp.bfloat16)] * 2,
        name="near_first",
        compiler_params=GRANT,
    )(keep(got), points, keep(mine))


def near_rest_kernel(
    points_ref, mine_ref, push_ref, source_ref, flags_ref, out_ref, high, low
):
    for blocks in ((1, 2), (3,)):
        totals = couple(blocks, points_ref, flags_ref, push_ref, source_ref, high, low)
        for where, block in enumerate(blocks):
            for comp in range(COMPS):
                value = totals[comp][:, 128 * where : 128 * where + 128]
                out_ref[block - 1, comp] = value + mine_ref[block, comp]


def near_rest(points, mine, push, source, flags):
    return pl.pallas_call(
        near_rest_kernel,
        out_shape=kept((BLOCKS_DEV - 1, COMPS, RHS, 128)),
        in_specs=[ON_CHIP] * 5,
        out_specs=ON_CHIP,
        scratch_shapes=[pltpu.VMEM((2, 6, 256, 256), jnp.bfloat16)] * 2,
        name="near_rest",
        compiler_params=GRANT,
    )(points, keep(mine), keep(push), keep(source), keep(flags))


def solve_kernel(panel, parts_ref, ih_ref, il_ref, out_ref):
    diag = parts_ref[0]
    for part in range(1, COLS):
        diag = diag + parts_ref[part]
    value = product(diag, ih_ref[panel], il_ref[panel])
    for quarter in range(4):
        out_ref[pl.ds(quarter, RHS, stride=4), :] = value[:, 128 * quarter : 128 * quarter + 128]


def add_kernel(got_ref, out_ref):
    total = got_ref[0:8]
    for at in range(1, 16):
        total = total + got_ref[8 * at : 8 * at + 8]
    total = total + pltpu.roll(total, 4, axis=0)
    for at in range(16):
        out_ref[8 * at : 8 * at + 8] = total


def solve(panel, parts, ih, il):
    partial = pl.pallas_call(
        functools.partial(solve_kernel, panel),
        out_shape=kept((RHS * 4, 128)),
        in_specs=[ON_CHIP] * 3,
        out_specs=ON_CHIP,
        name="solve",
        compiler_params=GRANT,
    )(keep(parts), keep(ih), keep(il))
    got = lax.all_to_all(partial.reshape(ROWS, 4, 128), "row", 0, 0, tiled=True)
    summed = pl.pallas_call(
        add_kernel,
        out_shape=kept((ROWS * 4, 128)),
        in_specs=[ON_CHIP],
        out_specs=ON_CHIP,
        name="add",
        compiler_params=GRANT,
    )(keep(got.reshape(ROWS * 4, 128)))
    got = lax.all_to_all(summed.reshape(ROWS, 4, 128), "row", 0, 0, tiled=True)
    return got.reshape(ROWS * 4, 128)


def whole(answer_ref):
    return jnp.concatenate(
        [answer_ref[pl.ds(quarter, RHS, stride=4), :] for quarter in range(4)], axis=1
    )


def diagonal_kernel(answer_ref, dh_ref, dl_ref, near_ref, out_ref):
    change = product(whole(answer_ref), dh_ref[...], dl_ref[...])
    value = near_ref[1] - change
    for part in range(COLS):
        out_ref[part] = value


def diagonal(answer, dh, dl, near):
    return pl.pallas_call(
        diagonal_kernel,
        out_shape=kept((COLS, RHS, 128)),
        in_specs=[ON_CHIP] * 4,
        out_specs=ON_CHIP,
        name="diagonal",
        compiler_params=GRANT,
    )(keep(answer), keep(dh), keep(dl), keep(near))


def changes(panel, answer_ref, fh_hbm, fl_hbm, high, low, read):
    count = 2 * COMPS
    copies = []
    for at in range(count):
        copies.append(pltpu.make_async_copy(fh_hbm.at[panel, at], high.at[at], read.at[at]))
        copies.append(pltpu.make_async_copy(fl_hbm.at[panel, at], low.at[at], read.at[count + at]))
    for copy in copies:
        copy.start()
    answer = whole(answer_ref)
    for comp in range(COMPS):
        for pair in range(2):
            at = 2 * comp + pair
            copies[2 * at].wait()
            copies[2 * at + 1].wait()
            value = product(answer, high[at], low[at])
            for where in range(2):
                block = 2 * pair + where
                hidden = block == 0 and comp <= panel
                yield block, comp, None if hidden else value[:, 128 * where : 128 * where + 128]


STREAM = [
    pltpu.VMEM((2 * COMPS, COLUMNS, 256), jnp.bfloat16),
    pltpu.VMEM((2 * COMPS, COLUMNS, 256), jnp.bfloat16),
    pltpu.SemaphoreType.DMA((4 * COMPS,)),
]


def change_first_kernel(answer_ref, fh_hbm, fl_hbm, first_ref, rest_ref, out_ref, *stream):
    for block, comp, value in changes(0, answer_ref, fh_hbm, fl_hbm, *stream):
        base = first_ref[comp] if block == 0 else rest_ref[block - 1, comp]
        out_ref[block, comp] = base if value is None else base - value


def change_first(answer, fh, fl, first, rest):
    return pl.pallas_call(
        change_first_kernel,
        out_shape=kept((BLOCKS_DEV, COMPS, RHS, 128)),
        in_specs=[ON_CHIP, IN_PLACE, IN_PLACE, ON_CHIP, ON_CHIP],
        out_specs=ON_CHIP,
        scratch_shapes=STREAM,
        name="change_first",
        compiler_params=GRANT,
    )(keep(answer), stay(fh), stay(fl), keep(first), keep(rest))


def change_second_kernel(answer_ref, fh_hbm, fl_hbm, base_ref, out_ref, *stream):
    for block, comp, value in changes(1, answer_ref, fh_hbm, fl_hbm, *stream):
        base = base_ref[block, comp]
        value = base if value is None else base - value
        for part in range(COLS):
            out_ref[part, block, comp] = value[SHARE * part : SHARE * part + SHARE]


def change_second(answer, fh, fl, base):
    return pl.pallas_call(
        change_second_kernel,
        out_shape=pltpu.HBM((COLS, BLOCKS_DEV, COMPS, SHARE, 128), jnp.float32),
        in_specs=[ON_CHIP, IN_PLACE, IN_PLACE, ON_CHIP],
        out_specs=ON_CHIP,
        scratch_shapes=STREAM,
        name="change_second",
        compiler_params=GRANT,
    )(keep(answer), stay(fh), stay(fl), keep(base))


def body(obstacles, particles, forces, neighbours, carried, factor, inverses):
    sent = payload(forces, particles, neighbours).reshape(ROWS * COLS, SHARE, 128)
    got = lax.all_to_all(sent, ("row", "col"), 0, 0, tiled=True).reshape(ROWS * RHS, 128)
    rows = factor.transpose(0, 1, 3, 2, 4).reshape(2, COLUMNS * COMPS * BLOCKS_DEV, 128)
    fh, fl, dh, dl, ih, il, mine = prepare(rows, inverses, carried)
    near0, spread, push, source, flags = near_first(got, obstacles, mine)
    parts = lax.all_to_all(spread, "col", 0, 0, tiled=True)
    rest = near_rest(obstacles, mine, push, source, flags)
    first = solve(0, parts, ih, il)
    first, rest = lax.optimization_barrier((first, rest))
    parts = lax.all_to_all(diagonal(first, dh, dl, near0), "col", 0, 0, tiled=True)
    part = change_first(first, fh, fl, near0, rest)
    second = solve(1, parts, ih, il)
    part = change_second(second, fh, fl, part)
    back = lax.all_to_all(part, "col", 0, 0, tiled=True)
    answers = jnp.stack([first.reshape(RHS, COLUMNS), second.reshape(RHS, COLUMNS)])
    return (answers, jnp.sum(back, axis=0))


def solution(mesh):
    in_specs = (
        P(None, "row"),
        P(None, "row"),
        P(None, None, "row"),
        P("row", "col"),
        P("row", None, None, None),
        P(None, "col", "row", None, None),
        P(None, "row", "col"),
    )
    out_specs = (P(None, None, "col"), P("row", None, "col", None))
    return jax.shard_map(body, mesh=mesh, in_specs=in_specs, out_specs=out_specs, check_vma=False)
```

profile of v0, /device:TPU:1, one launch (start us, length us, event | category | flops | bytes accessed | tf_op | source)
XLA Modules:
  0.0 129.2 jit_solution(8572865913467417539)
XLA Ops:
  0.6 2.1 %payload.1 = f32[32,8,4,128]{3,2,1,0:T(4,128)} custom-call(f32[3,32,256]{2,1,0:T(8,128)} %forces_hbm.1, f32[3,256]{1,0:T(4,128)} %particles_hbm.1, s32[2,4]{1,0:T(2,128)} %neighbours_hbm.1), custom_call_target="tpu_custom_call" | custom-call | tf_op jit(solution)/shard_map/payload/pallas_call | solution.py:96
  2.7 15.7 %all-to-all-start = ((f32[256,4,128]{2,1,0:T(4,128)}), f32[256,4,128]{2,1,0:T(4,128)S(1)}, u32[]{:S(2)}, u32[]{:S(2)}) async-start(f32[256,4,128]{2,1,0:T(4,128)} %bitcast.23), calls=%async_computation | async-start | bytes 1048576 | tf_op jit(solution)/shard_map/all_to_all | solution.py:413
  18.4 0.0 copy-start
  18.4 2.8 %copy-done = f32[2,512,4,3,128]{4,2,3,1,0:T(4,128)S(1)} copy-done((f32[2,512,4,3,128]{4,2,3,1,0:T(4,128)S(1)}, f32[2,512,4,3,128]{4,2,3,1,0:T(4,128)}, u32[]{:S(2)}) %copy-start) | copy-done | bytes 6291480
  21.1 0.0 copy-start.1
  21.1 1.0 copy-done.1
  22.2 0.0 copy-start.2
  22.2 0.9 copy-done.2
  23.1 0.0 copy-start.3
  23.1 4.0 %prepare.1 = (bf16[2,6,512,256]{3,2,1,0:T(8,128)(2,1)}, bf16[2,6,512,256]{3,2,1,0:T(8,128)(2,1)}, bf16[512,128]{1,0:T(8,128)(2,1)S(1)}, bf16[512,128]{1,0:T(8,12...) custom-call(f32[2,6144,128]{2,1,0:T(8,128)S(1)} %bitcast.13, ...), custom_call_target="tpu_custom_call" | custom-call | tf_op jit(solution)/shard_map/prepare/pallas_call | solution.py:141
  27.1 11.1 %all-to-all-done = f32[256,4,128]{2,1,0:T(4,128)S(1)} async-done(((f32[256,4,128]{2,1,0:T(4,128)}), f32[256,4,128]{2,1,0:T(4,128)S(1)}, u32[]{:S(2)}, u32[]{:S(2)}) %all-to-all-start) | async-done | bytes 524320 | tf_op jit(solution)/shard_map/all_to_all | solution.py:413
  38.2 0.0 copy-done.3
  38.2 2.1 %near_first.1 = (f32[3,32,128]{2,1,0:T(8,128)S(1)}, f32[8,32,128]{2,1,0:T(8,128)S(1)}, bf16[3,4,64,256]{3,2,1,0:T(8,128)(2,1)S(1)}, f32[3,1024,128]{2,1,0:T(8,128)S(1)}, f32[4,256]{1,0:T(4,128)S(1)}) custom-call(f32[1024,128]{1,0:T(8,128)S(1)} %bitcast.14, f32[3,512]{1,0:T(4,128)S(1)} %copy-done.3, f32[4,3,32,128]{3,2,1,0:T(8,128)S(1)} %get-tuple-element.16.mine_ref), custom_call_target="tpu_custom_call" | custom-call | tf_op jit(solution)/shard_map/near_first/pallas_call | solution.py:241
  40.3 9.7 %all_to_all.40.parts_ref = f32[8,32,128]{2,1,0:T(8,128)S(1)} all-to-all(f32[8,32,128]{2,1,0:T(8,128)S(1)} %get-tuple-element.17), channel_id=1, replica_groups=mesh['row'=32,'col'=8] {'col'}, dimensions={0} | all-to-all | bytes 262144 | tf_op jit(solution)/shard_map/all_to_all | solution.py:417
  50.1 0.1 solve.2
  50.2 11.9 %all_to_all.41 = f32[32,4,128]{2,1,0:T(4,128)S(1)} all-to-all(f32[32,4,128]{2,1,0:T(4,128)S(1)} %bitcast.22), channel_id=1, replica_groups=mesh['row'=32,'col'=8] {'row'}, dimensions={0} | all-to-all | bytes 131072 | tf_op jit(solution)/shard_map/all_to_all | solution.py:308
  62.1 0.7 add.2
  62.8 3.9 %all-to-all-start.3 = ((f32[32,4,128]{2,1,0:T(4,128)}), f32[32,4,128]{2,1,0:T(4,128)S(1)}, u32[]{:S(2)}, u32[]{:S(2)}) async-start(f32[32,4,128]{2,1,0:T(4,128)} %bitcast.6), calls=%async_computation.3 | async-start | bytes 131072 | tf_op jit(solution)/shard_map/all_to_all | solution.py:317
  66.6 4.1 %near_rest.1.rest_ref = f32[3,3,32,128]{3,2,1,0:T(8,128)S(1)} custom-call(f32[3,512]{1,0:T(4,128)S(1)} %copy-done.3, f32[4,3,32,128]{3,2,1,0:T(8,128)S(1)} %get-tuple-element.16.mine_ref, bf16[3,4,64,256]{3,2,1,0:T(8,128)(2,1)S(1)} %get-tuple-element.20.push_ref, f32[3,1024,128]{2,1,0:T(8,128)S(1)} %get-tuple-element.21.source_ref, ...), custom_call_target="tpu_custom_call" | custom-call | tf_op jit(solution)/shard_map/near_rest/pallas_call | solution.py:270
  70.8 4.7 %all-to-all-done.3 = f32[32,4,128]{2,1,0:T(4,128)S(1)} async-done(((f32[32,4,128]{2,1,0:T(4,128)}), f32[32,4,128]{2,1,0:T(4,128)S(1)}, u32[]{:S(2)}, u32[]{:S(2)}) %all-to-all-start.3) | async-done | bytes 65568 | tf_op jit(solution)/shard_map/all_to_all | solution.py:317
  75.5 0.2 diagonal.1
  75.7 11.0 %all_to_all.42.parts_ref = f32[8,32,128]{2,1,0:T(8,128)S(1)} all-to-all(f32[8,32,128]{2,1,0:T(8,128)S(1)} %diagonal.1), channel_id=1, replica_groups=mesh['row'=32,'col'=8] {'col'}, dimensions={0} | all-to-all | bytes 262144 | tf_op jit(solution)/shard_map/all_to_all | solution.py:421
  86.7 0.1 solve.3
  86.9 12.3 %all_to_all.43 = f32[32,4,128]{2,1,0:T(4,128)S(1)} all-to-all(f32[32,4,128]{2,1,0:T(4,128)S(1)} %bitcast.21), channel_id=1, replica_groups=mesh['row'=32,'col'=8] {'row'}, dimensions={0} | all-to-all | bytes 131072 | tf_op jit(solution)/shard_map/all_to_all | solution.py:308
  99.2 0.7 add.3
  99.8 3.9 %all-to-all-start.6 = ((f32[32,4,128]{2,1,0:T(4,128)}), f32[32,4,128]{2,1,0:T(4,128)S(1)}, u32[]{:S(2)}, u32[]{:S(2)}) async-start(f32[32,4,128]{2,1,0:T(4,128)} %bitcast.10), calls=%async_computation.6 | async-start | bytes 131072 | tf_op jit(solution)/shard_map/all_to_all | solution.py:317
  103.7 2.7 %change_first.1.base_ref = f32[4,3,32,128]{3,2,1,0:T(8,128)S(1)} custom-call(f32[128,128]{1,0:T(8,128)S(1)} %bitcast.16, bf16[2,6,512,256]{3,2,1,0:T(8,128)(2,1)} %get-tuple-element.27.fh_hbm, bf16[2,6,512,256]{3,2,1,0:T(8,128)(2,1)} %get-tuple-element.28.fl_hbm, f32[3,32,128]{2,1,0:T(8,128)S(1)} %get-tuple-element.26.near_ref.first_ref, ...), custom_call_target="tpu_custom_call" | custom-call | tf_op jit(solution)/shard_map/change_first/pallas_call | solution.py:380
  106.4 6.1 %all-to-all-done.6 = f32[32,4,128]{2,1,0:T(4,128)S(1)} async-done(((f32[32,4,128]{2,1,0:T(4,128)}), f32[32,4,128]{2,1,0:T(4,128)S(1)}, u32[]{:S(2)}, u32[]{:S(2)}) %all-to-all-start.6) | async-done | bytes 65568 | tf_op jit(solution)/shard_map/all_to_all | solution.py:317
  112.6 3.4 %change_second.1 = f32[8,4,3,4,128]{4,3,2,1,0:T(4,128)} custom-call(f32[128,128]{1,0:T(8,128)S(1)} %bitcast.18, bf16[2,6,512,256]{3,2,1,0:T(8,128)(2,1)} %get-tuple-element.27.fh_hbm, bf16[2,6,512,256]{3,2,1,0:T(8,128)(2,1)} %get-tuple-element.28.fl_hbm, f32[4,3,32,128]{3,2,1,0:T(8,128)S(1)} %change_first.1.base_ref), custom_call_target="tpu_custom_call" | custom-call | tf_op jit(solution)/shard_map/change_second/pallas_call | solution.py:400
  116.0 6.7 %all-to-all-start.7 = ((f32[8,4,3,4,128]{4,3,2,1,0:T(4,128)}), f32[8,4,3,4,128]{4,3,2,1,0:T(4,128)S(1)}, u32[]{:S(2)}, u32[]{:S(2)}) async-start(f32[8,4,3,4,128]{4,3,2,1,0:T(4,128)} %change_second.1), calls=%async_computation.7 | async-start | bytes 393216 | tf_op jit(solution)/shard_map/all_to_all | solution.py:425
  122.7 0.7 pad_maximum_fusion
  123.4 5.2 %all-to-all-done.7 = f32[8,4,3,4,128]{4,3,2,1,0:T(4,128)S(1)} async-done(((f32[8,4,3,4,128]{4,3,2,1,0:T(4,128)}), f32[8,4,3,4,128]{4,3,2,1,0:T(4,128)S(1)}, u32[]{:S(2)}, u32[]{:S(2)}) %all-to-all-start.7) | async-done | bytes 196640 | tf_op jit(solution)/shard_map/all_to_all | solution.py:425
  128.6 0.6 reduce_sum.9
  (2 shorter events, 0.0 us)
Async XLA Ops:
  2.7 35.5 %all-to-all-start = ((f32[256,4,128]{2,1,0:T(4,128)}), f32[256,4,128]{2,1,0:T(4,128)S(1)}, u32[]{:S(2)}, u32[]{:S(2)}) async-start(f32[256,4,128]{2,1,0:T(4,128)} %bitcast.23), calls=%async_computation | async-start | bytes 1048576 | tf_op jit(solution)/shard_map/all_to_all | solution.py:413
  18.4 2.8 %copy-start = (f32[2,512,4,3,128]{4,2,3,1,0:T(4,128)S(1)}, f32[2,512,4,3,128]{4,2,3,1,0:T(4,128)}, u32[]{:S(2)}) copy-start(f32[2,512,4,3,128]{4,2,3,1,0:T(4,128)} %param.12) | copy-start | bytes 18874372
  21.1 1.0 copy-start.1
  22.2 0.9 copy-start.2
  23.1 15.1 %copy-start.3 = (f32[3,512]{1,0:T(4,128)S(1)}, f32[3,512]{1,0:T(4,128)}, u32[]{:S(2)}) copy-start(f32[3,512]{1,0:T(4,128)} %points_ref.3) | copy-start | bytes 18436
  62.8 12.7 %all-to-all-start.3 = ((f32[32,4,128]{2,1,0:T(4,128)}), f32[32,4,128]{2,1,0:T(4,128)S(1)}, u32[]{:S(2)}, u32[]{:S(2)}) async-start(f32[32,4,128]{2,1,0:T(4,128)} %bitcast.6), calls=%async_computation.3 | async-start | bytes 131072 | tf_op jit(solution)/shard_map/all_to_all | solution.py:317
  99.8 12.7 %all-to-all-start.6 = ((f32[32,4,128]{2,1,0:T(4,128)}), f32[32,4,128]{2,1,0:T(4,128)S(1)}, u32[]{:S(2)}, u32[]{:S(2)}) async-start(f32[32,4,128]{2,1,0:T(4,128)} %bitcast.10), calls=%async_computation.6 | async-start | bytes 131072 | tf_op jit(solution)/shard_map/all_to_all | solution.py:317
  116.0 12.6 %all-to-all-start.7 = ((f32[8,4,3,4,128]{4,3,2,1,0:T(4,128)}), f32[8,4,3,4,128]{4,3,2,1,0:T(4,128)S(1)}, u32[]{:S(2)}, u32[]{:S(2)}) async-start(f32[8,4,3,4,128]{4,3,2,1,0:T(4,128)} %change_second.1), calls=%async_computation.7 | async-start | bytes 393216 | tf_op jit(solution)/shard_map/all_to_all | solution.py:425
where the time goes:
time: 130 us; the launch traced here: 129 us
  blocking collectives  45 us (35%)
  starting transfers between devices  30.1 us (23%)
  waiting for transfers between devices  27.2 us (21%)
  Pallas kernels  20.2 us (16%)
  local copies, waits for them, and re-layouts  4.79 us (4%)
  other arithmetic  1.31 us (1%)
    all_to_all x2, blocking collectives, solve(): got = lax.all_to_all(partial.reshape(ROWS, 4, 128), 'row', 0, 0, tiled=True)  24.2 us
    all_to_all x1, starting transfers between devices, body(): lax.all_to_all(sent, ('row', 'col'), 0, 0, tiled=True)  15.7 us
    all_to_all x1, waiting for transfers between devices, body(): lax.all_to_all(sent, ('row', 'col'), 0, 0, tiled=True)  11.1 us
    all_to_all x1, blocking collectives, body(): lax.all_to_all(diagonal(first, dh, dl, near0), 'col', 0, 0, tiled=True)  11 us
    all_to_all x2, waiting for transfers between devices, solve(): got = lax.all_to_all(summed.reshape(ROWS, 4, 128), 'row', 0, 0, tiled=True)  10.9 us
    all_to_all x1, blocking collectives, body(): parts = lax.all_to_all(spread, 'col', 0, 0, tiled=True)  9.74 us
    all_to_all x2, starting transfers between devices, solve(): got = lax.all_to_all(summed.reshape(ROWS, 4, 128), 'row', 0, 0, tiled=True)  7.71 us
    all_to_all x1, starting transfers between devices, body(): back = lax.all_to_all(part, 'col', 0, 0, tiled=True)  6.73 us
  transfers between devices with their start and end apart: 4, of which 4 were waited for; matrix products, arithmetic and copies ran while one was open for 1% of the time, Pallas kernels for 8%

commit v1 on v0

--- a/solution.py
+++ b/solution.py
@@ -16,6 +16,9 @@
 PAIRS = ((0, 0), (1, 1), (2, 2), (0, 1), (0, 2), (1, 2))
 SHARE = RHS // COLS
 COLUMNS = 512
+RING = 4
+DEPTH = 8
+EIGHT = RHS // RING
 
 ON_CHIP = pl.BlockSpec(memory_space=pltpu.VMEM)
 IN_PLACE = pl.BlockSpec(memory_space=pltpu.HBM)
@@ -111,24 +114,25 @@
     )(stay(forces), stay(particles), stay(neighbours))
 
 
-def prepare_kernel(
-    factor_ref, inverses_ref, carried_ref, fh_ref, fl_ref, dh_ref, dl_ref, ih_ref, il_ref, mine_ref
-):
+def prepare_kernel(factor_ref, inverses_ref, carried_ref, fh_ref, fl_ref, lend_ref, ih_ref, il_ref, mine_ref):
     for panel in range(2):
         for comp in range(COMPS):
             for block in range(BLOCKS_DEV):
                 rows = pl.ds(BLOCKS_DEV * comp + block, COLUMNS, stride=COMPS * BLOCKS_DEV)
-                high, low = halves(factor_ref[panel, rows, :])
+                value = factor_ref[panel, rows, :]
+                high, low = halves(value)
                 pair = 2 * comp + block // 2
                 lanes = pl.ds(128 * (block % 2), 128)
                 fh_ref[panel, pair, :, lanes] = high
                 fl_ref[panel, pair, :, lanes] = low
                 if panel == 0 and comp == 1 and block == 0:
-                    dh_ref[...] = high
-                    dl_ref[...] = low
-        high, low = halves(inverses_ref[panel])
-        ih_ref[panel] = high
-        il_ref[panel] = low
+                    for quarter in range(4):
+                        lend_ref[quarter] = value[128 * quarter : 128 * quarter + 128]
+    for quarter in range(4):
+        lend_ref[4 + quarter] = inverses_ref[1, :, pl.ds(128 * quarter, 128)]
+    high, low = halves(inverses_ref[0])
+    ih_ref[...] = high
+    il_ref[...] = low
     owner = lax.broadcasted_iota(jnp.int32, (RHS, 128), 0) // SHARE
     own = owner == jnp.full((RHS, 128), lax.axis_index("col"), jnp.int32)
     for block in range(BLOCKS_DEV):
@@ -143,17 +147,23 @@
         out_shape=(
             pltpu.HBM(panels, jnp.bfloat16),
             pltpu.HBM(panels, jnp.bfloat16),
-            kept((COLUMNS, 128), jnp.bfloat16),
-            kept((COLUMNS, 128), jnp.bfloat16),
-            kept(inverses.shape, jnp.bfloat16),
-            kept(inverses.shape, jnp.bfloat16),
+            pltpu.HBM((8, 128, 128), jnp.float32),
+            kept((128, COLUMNS), jnp.bfloat16),
+            kept((128, COLUMNS), jnp.bfloat16),
             kept(carried.shape),
         ),
         in_specs=[ON_CHIP] * 3,
-        out_specs=(ON_CHIP,) * 7,
+        out_specs=(ON_CHIP,) * 6,
         name="prepare",
         compiler_params=GRANT,
     )(factor_rows, inverses, carried)
+
+
+def fill(places_ref, source):
+    for comp in range(COMPS):
+        for group in range(ROWS):
+            column = places_ref[comp, :, group : group + 1]
+            source[comp, pl.ds(SLICE * group, SLICE), :] = jnp.broadcast_to(column, (SLICE, 128))
 
 
 def couple(blocks, points_ref, flags_ref, push_ref, source_ref, high, low):
@@ -200,7 +210,7 @@
 
 
 def near_first_kernel(
-    got_ref, points_ref, mine_ref, out_ref, spread_ref, push_ref, source_ref, flags_ref, high, low
+    got_ref, points_ref, mine_ref, out_ref, spread_ref, push_ref, places_ref, flags_ref, source_ref, high, low
 ):
     lane = lax.broadcasted_iota(jnp.int32, (RHS, 128), 1) // SLICE
     for quad in range(8):
@@ -216,10 +226,8 @@
             push_ref[comp, quad // 2, 0:32, lanes] = top
             push_ref[comp, quad // 2, 32:64, lanes] = rest
     for comp in range(COMPS):
-        places = got_ref[pl.ds(comp, ROWS, stride=RHS), :].T
-        for group in range(ROWS):
-            column = places[96:128, group : group + 1]
-            source_ref[comp, pl.ds(SLICE * group, SLICE), :] = jnp.broadcast_to(column, (SLICE, 128))
+        places_ref[comp] = got_ref[pl.ds(comp, ROWS, stride=RHS), :].T[96:128, :]
+    fill(places_ref, source_ref)
     lists = got_ref[pl.ds(3, ROWS * COLS, stride=4), :].T[96:104, :]
     first = BLOCKS_DEV * lax.axis_index("row")
     for block in range(BLOCKS_DEV):
@@ -244,20 +252,22 @@
             kept((COMPS, RHS, 128)),
             kept((COLS, RHS, 128)),
             kept((COMPS, 4, 64, 256), jnp.bfloat16),
-            kept((COMPS, ROWS * SLICE, 128)),
+            kept((COMPS, SLICE, ROWS)),
             kept((BLOCKS_DEV, 256)),
         ),
         in_specs=[ON_CHIP] * 3,
         out_specs=(ON_CHIP,) * 5,
-        scratch_shapes=[pltpu.VMEM((2, 6, 256, 128), jnp.bfloat16)] * 2,
+        scratch_shapes=[pltpu.VMEM((COMPS, ROWS * SLICE, 128), jnp.float32)]
+        + [pltpu.VMEM((2, 6, 256, 128), jnp.bfloat16)] * 2,
         name="near_first",
         compiler_params=GRANT,
     )(keep(got), points, keep(mine))
 
 
 def near_rest_kernel(
-    points_ref, mine_ref, push_ref, source_ref, flags_ref, out_ref, high, low
+    points_ref, mine_ref, push_ref, places_ref, flags_ref, out_ref, source_ref, high, low
 ):
+    fill(places_ref, source_ref)
     for blocks in ((1, 2), (3,)):
         totals = couple(blocks, points_ref, flags_ref, push_ref, source_ref, high, low)
         for where, block in enumerate(blocks):
@@ -266,165 +276,227 @@
                 out_ref[block - 1, comp] = value + mine_ref[block, comp]
 
 
-def near_rest(points, mine, push, source, flags):
+def near_rest(points, mine, push, places, flags):
     return pl.pallas_call(
         near_rest_kernel,
         out_shape=kept((BLOCKS_DEV - 1, COMPS, RHS, 128)),
         in_specs=[ON_CHIP] * 5,
         out_specs=ON_CHIP,
-        scratch_shapes=[pltpu.VMEM((2, 6, 256, 256), jnp.bfloat16)] * 2,
+        scratch_shapes=[pltpu.VMEM((COMPS, ROWS * SLICE, 128), jnp.float32)]
+        + [pltpu.VMEM((2, 6, 256, 256), jnp.bfloat16)] * 2,
         name="near_rest",
         compiler_params=GRANT,
-    )(points, keep(mine), keep(push), keep(source), keep(flags))
-
-
-def solve_kernel(panel, parts_ref, ih_ref, il_ref, out_ref):
-    diag = parts_ref[0]
-    for part in range(1, COLS):
-        diag = diag + parts_ref[part]
-    value = product(diag, ih_ref[panel], il_ref[panel])
+    )(points, keep(mine), keep(push), keep(places), keep(flags))
+
+
+def total(parts_ref):
+    value = parts_ref[0]
+    for part in range(1, parts_ref.shape[0]):
+        value = value + parts_ref[part]
+    return value
+
+
+def first_solve_kernel(parts_ref, ih_ref, il_ref, near_ref, out_ref):
+    value = product(total(parts_ref), ih_ref[...], il_ref[...])
+    for y in range(RING):
+        sides = slice(EIGHT * y, EIGHT * y + EIGHT)
+        for quarter in range(4):
+            out_ref[y, pl.ds(EIGHT * quarter, EIGHT), :] = value[sides, 128 * quarter : 128 * quarter + 128]
+        out_ref[y, pl.ds(32, EIGHT), :] = near_ref[1, pl.ds(EIGHT * y, EIGHT), :]
+
+
+def first_solve(parts, ih, il, near):
+    return pl.pallas_call(
+        first_solve_kernel,
+        out_shape=kept((RING, 40, 128)),
+        in_specs=[ON_CHIP] * 4,
+        out_specs=ON_CHIP,
+        name="first_solve",
+        compiler_params=GRANT,
+    )(keep(parts), keep(ih), keep(il), keep(near))
+
+
+def add_kernel(got_ref, out_ref):
+    value = total(got_ref)[0:32]
+    for part in range(DEPTH):
+        out_ref[part] = value
+
+
+def add(got):
+    return pl.pallas_call(
+        add_kernel,
+        out_shape=kept((DEPTH, 32, 128)),
+        in_specs=[ON_CHIP],
+        out_specs=ON_CHIP,
+        name="add",
+        compiler_params=GRANT,
+    )(keep(got))
+
+
+def wide(value):
+    return jnp.concatenate([value[EIGHT * q : EIGHT * q + EIGHT] for q in range(4)], axis=1)
+
+
+def diagonal_kernel(parts_ref, got_ref, own_ref, one_ref, two_ref, three_ref, answer_ref, out_ref):
+    value = total(parts_ref)
+    answer_ref[...] = value
+    answer = wide(value)
+    y = lax.axis_index("row") % RING
+    for step, tiles in enumerate((own_ref, one_ref, two_ref, three_ref)):
+        columns = jnp.concatenate([tiles[quarter] for quarter in range(4)], axis=0)
+        base = got_ref[(y + step) % RING, pl.ds(32, EIGHT), :]
+        value = base - product(answer, *halves(columns))
+        for part in range(COLS):
+            out_ref[part, pl.ds(EIGHT * step, EIGHT), :] = value
+
+
+def diagonal(parts, got, tiles):
+    return pl.pallas_call(
+        diagonal_kernel,
+        out_shape=(kept((32, 128)), kept((COLS, 32, 128))),
+        in_specs=[ON_CHIP] * 6,
+        out_specs=(ON_CHIP,) * 2,
+        name="diagonal",
+        compiler_params=GRANT,
+    )(keep(parts), keep(got), *[keep(tile) for tile in tiles])
+
+
+def second_solve_kernel(parts_ref, own_ref, one_ref, two_ref, three_ref, out_ref):
+    diag = total(parts_ref)
+    value = None
+    for step, tiles in enumerate((own_ref, one_ref, two_ref, three_ref)):
+        inverse = jnp.concatenate([tiles[4 + quarter] for quarter in range(4)], axis=1)
+        add = product(diag[EIGHT * step : EIGHT * step + EIGHT], *halves(inverse))
+        value = add if value is None else value + add
+    for part in range(DEPTH):
+        for quarter in range(4):
+            out_ref[part, pl.ds(EIGHT * quarter, EIGHT), :] = value[:, 128 * quarter : 128 * quarter + 128]
+
+
+def second_solve(parts, tiles):
+    return pl.pallas_call(
+        second_solve_kernel,
+        out_shape=kept((DEPTH, 32, 128)),
+        in_specs=[ON_CHIP] * 5,
+        out_specs=ON_CHIP,
+        name="second_solve",
+        compiler_params=GRANT,
+    )(keep(parts), *[keep(tile) for tile in tiles])
+
+
+def gather_kernel(parts_ref, first_ref, out_ref):
+    second = total(parts_ref)
+    for y in range(RING):
+        out_ref[y, 0:32] = first_ref[...]
+        out_ref[y, 32:64] = second
+
+
+def gather(parts, first):
+    return pl.pallas_call(
+        gather_kernel,
+        out_shape=kept((RING, 64, 128)),
+        in_specs=[ON_CHIP] * 2,
+        out_specs=ON_CHIP,
+        name="gather",
+        compiler_params=GRANT,
+    )(keep(parts), keep(first))
+
+
+def whole(got_ref, panel):
+    columns = []
     for quarter in range(4):
-        out_ref[pl.ds(quarter, RHS, stride=4), :] = value[:, 128 * quarter : 128 * quarter + 128]
-
-
-def add_kernel(got_ref, out_ref):
-    total = got_ref[0:8]
-    for at in range(1, 16):
-        total = total + got_ref[8 * at : 8 * at + 8]
-    total = total + pltpu.roll(total, 4, axis=0)
-    for at in range(16):
-        out_ref[8 * at : 8 * at + 8] = total
-
-
-def solve(panel, parts, ih, il):
-    partial = pl.pallas_call(
-        functools.partial(solve_kernel, panel),
-        out_shape=kept((RHS * 4, 128)),
-        in_specs=[ON_CHIP] * 3,
-        out_specs=ON_CHIP,
-        name="solve",
-        compiler_params=GRANT,
-    )(keep(parts), keep(ih), keep(il))
-    got = lax.all_to_all(partial.reshape(ROWS, 4, 128), "row", 0, 0, tiled=True)
-    summed = pl.pallas_call(
-        add_kernel,
-        out_shape=kept((ROWS * 4, 128)),
+        rows = pl.ds(32 * panel + EIGHT * quarter, EIGHT)
+        columns.append(jnp.concatenate([got_ref[y, rows, :] for y in range(RING)], axis=0))
+    return jnp.concatenate(columns, axis=1)
+
+
+def answers_kernel(got_ref, out_ref):
+    for panel in range(2):
+        out_ref[panel] = whole(got_ref, panel)
+
+
+def answers(got):
+    return pl.pallas_call(
+        answers_kernel,
+        out_shape=jax.ShapeDtypeStruct((2, RHS, COLUMNS), jnp.float32),
         in_specs=[ON_CHIP],
         out_specs=ON_CHIP,
-        name="add",
-        compiler_params=GRANT,
-    )(keep(got.reshape(ROWS * 4, 128)))
-    got = lax.all_to_all(summed.reshape(ROWS, 4, 128), "row", 0, 0, tiled=True)
-    return got.reshape(ROWS * 4, 128)
-
-
-def whole(answer_ref):
-    return jnp.concatenate(
-        [answer_ref[pl.ds(quarter, RHS, stride=4), :] for quarter in range(4)], axis=1
-    )
-
-
-def diagonal_kernel(answer_ref, dh_ref, dl_ref, near_ref, out_ref):
-    change = product(whole(answer_ref), dh_ref[...], dl_ref[...])
-    value = near_ref[1] - change
-    for part in range(COLS):
-        out_ref[part] = value
-
-
-def diagonal(answer, dh, dl, near):
-    return pl.pallas_call(
-        diagonal_kernel,
-        out_shape=kept((COLS, RHS, 128)),
-        in_specs=[ON_CHIP] * 4,
-        out_specs=ON_CHIP,
-        name="diagonal",
-        compiler_params=GRANT,
-    )(keep(answer), keep(dh), keep(dl), keep(near))
-
-
-def changes(panel, answer_ref, fh_hbm, fl_hbm, high, low, read):
-    count = 2 * COMPS
+        name="answers",
+        compiler_params=GRANT,
+    )(keep(got))
+
+
+def change_kernel(got_ref, fh_hbm, fl_hbm, first_ref, rest_ref, out_ref, high, low, read):
+    count = 4 * COMPS
     copies = []
     for at in range(count):
-        copies.append(pltpu.make_async_copy(fh_hbm.at[panel, at], high.at[at], read.at[at]))
-        copies.append(pltpu.make_async_copy(fl_hbm.at[panel, at], low.at[at], read.at[count + at]))
+        panel, pair = at % 2, at // 2
+        copies.append(pltpu.make_async_copy(fh_hbm.at[panel, pair], high.at[at], read.at[at]))
+        copies.append(pltpu.make_async_copy(fl_hbm.at[panel, pair], low.at[at], read.at[count + at]))
     for copy in copies:
         copy.start()
-    answer = whole(answer_ref)
+    sides = [whole(got_ref, panel) for panel in range(2)]
     for comp in range(COMPS):
         for pair in range(2):
-            at = 2 * comp + pair
-            copies[2 * at].wait()
-            copies[2 * at + 1].wait()
-            value = product(answer, high[at], low[at])
+            moved = []
+            for panel in range(2):
+                at = 2 * (2 * comp + pair) + panel
+                copies[2 * at].wait()
+                copies[2 * at + 1].wait()
+                moved.append(product(sides[panel], high[at], low[at]))
             for where in range(2):
                 block = 2 * pair + where
-                hidden = block == 0 and comp <= panel
-                yield block, comp, None if hidden else value[:, 128 * where : 128 * where + 128]
-
-
-STREAM = [
-    pltpu.VMEM((2 * COMPS, COLUMNS, 256), jnp.bfloat16),
-    pltpu.VMEM((2 * COMPS, COLUMNS, 256), jnp.bfloat16),
-    pltpu.SemaphoreType.DMA((4 * COMPS,)),
-]
-
-
-def change_first_kernel(answer_ref, fh_hbm, fl_hbm, first_ref, rest_ref, out_ref, *stream):
-    for block, comp, value in changes(0, answer_ref, fh_hbm, fl_hbm, *stream):
-        base = first_ref[comp] if block == 0 else rest_ref[block - 1, comp]
-        out_ref[block, comp] = base if value is None else base - value
-
-
-def change_first(answer, fh, fl, first, rest):
-    return pl.pallas_call(
-        change_first_kernel,
-        out_shape=kept((BLOCKS_DEV, COMPS, RHS, 128)),
+                value = first_ref[comp] if block == 0 else rest_ref[block - 1, comp]
+                for panel in range(2):
+                    if block > 0 or comp > panel:
+                        value = value - moved[panel][:, 128 * where : 128 * where + 128]
+                for part in range(COLS):
+                    out_ref[part, block, comp] = value[SHARE * part : SHARE * part + SHARE]
+
+
+def change(got, fh, fl, first, rest):
+    return pl.pallas_call(
+        change_kernel,
+        out_shape=pltpu.HBM((COLS, BLOCKS_DEV, COMPS, SHARE, 128), jnp.float32),
         in_specs=[ON_CHIP, IN_PLACE, IN_PLACE, ON_CHIP, ON_CHIP],
         out_specs=ON_CHIP,
-        scratch_shapes=STREAM,
-        name="change_first",
-        compiler_params=GRANT,
-    )(keep(answer), stay(fh), stay(fl), keep(first), keep(rest))
-
-
-def change_second_kernel(answer_ref, fh_hbm, fl_hbm, base_ref, out_ref, *stream):
-    for block, comp, value in changes(1, answer_ref, fh_hbm, fl_hbm, *stream):
-        base = base_ref[block, comp]
-        value = base if value is None else base - value
-        for part in range(COLS):
-            out_ref[part, block, comp] = value[SHARE * part : SHARE * part + SHARE]
-
-
-def change_second(answer, fh, fl, base):
-    return pl.pallas_call(
-        change_second_kernel,
-        out_shape=pltpu.HBM((COLS, BLOCKS_DEV, COMPS, SHARE, 128), jnp.float32),
-        in_specs=[ON_CHIP, IN_PLACE, IN_PLACE, ON_CHIP],
-        out_specs=ON_CHIP,
-        scratch_shapes=STREAM,
-        name="change_second",
-        compiler_params=GRANT,
-    )(keep(answer), stay(fh), stay(fl), keep(base))
+        scratch_shapes=[
+            pltpu.VMEM((4 * COMPS, COLUMNS, 256), jnp.bfloat16),
+            pltpu.VMEM((4 * COMPS, COLUMNS, 256), jnp.bfloat16),
+            pltpu.SemaphoreType.DMA((8 * COMPS,)),
+        ],
+        name="change",
+        compiler_params=GRANT,
+    )(keep(got), stay(fh), stay(fl), keep(first), keep(rest))
+
+
+def along(array, groups):
+    return lax.all_to_all(array, "row", 0, 0, axis_index_groups=groups, tiled=True)
 
 
 def body(obstacles, particles, forces, neighbours, carried, factor, inverses):
+    ring = [[RING * z + y for y in range(RING)] for z in range(DEPTH)]
+    line = [[RING * z + y for z in range(DEPTH)] for y in range(RING)]
     sent = payload(forces, particles, neighbours).reshape(ROWS * COLS, SHARE, 128)
     got = lax.all_to_all(sent, ("row", "col"), 0, 0, tiled=True).reshape(ROWS * RHS, 128)
     rows = factor.transpose(0, 1, 3, 2, 4).reshape(2, COLUMNS * COMPS * BLOCKS_DEV, 128)
-    fh, fl, dh, dl, ih, il, mine = prepare(rows, inverses, carried)
-    near0, spread, push, source, flags = near_first(got, obstacles, mine)
+    fh, fl, lend, ih, il, mine = prepare(rows, inverses, carried)
+    tiles = [lend]
+    for step in range(1, RING):
+        pairs = [(RING * z + (y + step) % RING, RING * z + y) for z in range(DEPTH) for y in range(RING)]
+        tiles.append(lax.ppermute(lend, "row", pairs))
+    near0, spread, push, places, flags = near_first(got, obstacles, mine)
     parts = lax.all_to_all(spread, "col", 0, 0, tiled=True)
-    rest = near_rest(obstacles, mine, push, source, flags)
-    first = solve(0, parts, ih, il)
-    first, rest = lax.optimization_barrier((first, rest))
-    parts = lax.all_to_all(diagonal(first, dh, dl, near0), "col", 0, 0, tiled=True)
-    part = change_first(first, fh, fl, near0, rest)
-    second = solve(1, parts, ih, il)
-    part = change_second(second, fh, fl, part)
-    back = lax.all_to_all(part, "col", 0, 0, tiled=True)
-    answers = jnp.stack([first.reshape(RHS, COLUMNS), second.reshape(RHS, COLUMNS)])
-    return (answers, jnp.sum(back, axis=0))
+    rest = near_rest(obstacles, mine, push, places, flags)
+    shares = along(first_solve(parts, ih, il, near0), ring)
+    parts = along(add(shares), line)
+    parts, rest = lax.optimization_barrier((parts, rest))
+    first, spread = diagonal(parts, shares, tiles)
+    parts = lax.all_to_all(spread, "col", 0, 0, tiled=True)
+    parts = along(second_solve(parts, tiles), line)
+    shares = along(gather(parts, first), ring)
+    back = lax.all_to_all(change(shares, fh, fl, near0, rest), "col", 0, 0, tiled=True)
+    return (answers(shares), jnp.sum(back, axis=0))
 
 
 def solution(mesh):

time: 130 us -> 122 us (0.938)
  waiting for transfers between devices: 27.2 us -> 13.7 us
  starting transfers between devices: 30.1 us -> 33.5 us
  blocking collectives: 45 us -> 47.2 us
    all_to_all x1 -> x2, blocking collectives: 9.74 us -> 21.3 us  [body(): parts = lax.all_to_all(spread, 'col', 0, 0, tiled=True)]
    all_to_all x3, blocking collectives: 35.2 us -> 25.9 us  [along(): lax.all_to_all(array, 'row', 0, 0, axis_index_groups=groups, tiled=True)]
    all_to_all x3 -> x2, waiting for transfers between devices: 16 us -> 7.46 us  [the longest x1 5.22 us: body(): lax.all_to_all(change(shares, fh, fl, near0, rest), 'col', 0, 0, tiled=True)]
    ppermute x0 -> x3, starting transfers between devices: none -> 4.93 us  [body(): tiles.append(lax.ppermute(lend, 'row', pairs))]
    all_to_all x1, waiting for transfers between devices: 11.1 us -> 6.22 us  [body(): lax.all_to_all(sent, ('row', 'col'), 0, 0, tiled=True)]
    all_to_all x3 -> x2, starting transfers between devices: 14.4 us -> 12.9 us  [the longest x1 7.11 us: body(): lax.all_to_all(change(shares, fh, fl, near0, rest), 'col', 0, 0, tiled=True)]
    unnamed x8 -> x14, local copies, waits for them, and re-layouts: 4.75 us -> 5.55 us
  transfers between devices with their start and end apart: 4 -> 6, of which waited for: 4 -> 3; matrix products, arithmetic and copies ran while one was open for 1% -> 0% of each run, Pallas kernels for 8% -> 10%
where the time goes in v1:
time: 122 us; the launch traced here: 121 us
  blocking collectives  47.2 us (39%)
  starting transfers between devices  33.5 us (27%)
  Pallas kernels  19.9 us (16%)
  waiting for transfers between devices  13.7 us (11%)
  local copies, waits for them, and re-layouts  5.55 us (5%)
    all_to_all x3, blocking collectives, along(): lax.all_to_all(array, 'row', 0, 0, axis_index_groups=groups, tiled=True)  25.9 us
    all_to_all x2, blocking collectives, body(): parts = lax.all_to_all(spread, 'col', 0, 0, tiled=True)  21.3 us
    all_to_all x1, starting transfers between devices, body(): lax.all_to_all(sent, ('row', 'col'), 0, 0, tiled=True)  15.7 us
    all_to_all x1, starting transfers between devices, body(): lax.all_to_all(change(shares, fh, fl, near0, rest), 'col', 0, 0, tiled=True)  7.11 us
    all_to_all x1, waiting for transfers between devices, body(): lax.all_to_all(sent, ('row', 'col'), 0, 0, tiled=True)  6.22 us
    all_to_all x1, starting transfers between devices, along(): lax.all_to_all(array, 'row', 0, 0, axis_index_groups=groups, tiled=True)  5.79 us
    unnamed x14, local copies, waits for them, and re-layouts  5.55 us
    all_to_all x1, waiting for transfers between devices, body(): lax.all_to_all(change(shares, fh, fl, near0, rest), 'col', 0, 0, tiled=True)  5.22 us
  transfers between devices with their start and end apart: 6, of which 3 were waited for; matrix products, arithmetic and copies ran while one was open for 0% of the time, Pallas kernels for 10%

profile of v1, /device:TPU:1, one launch (start us, length us, event | category | flops | bytes accessed | tf_op | source)
XLA Modules:
  0.0 121.2 jit_solution(7065791595957127953)
XLA Ops:
  0.6 2.0 %payload.1 = f32[32,8,4,128]{3,2,1,0:T(4,128)} custom-call(f32[3,32,256]{2,1,0:T(8,128)} %forces_hbm.1, f32[3,256]{1,0:T(4,128)} %particles_hbm.1, s32[2,4]{1,0:T(2,128)} %neighbours_hbm.1), custom_call_target="tpu_custom_call" | custom-call | tf_op jit(solution)/shard_map/payload/pallas_call | solution.py:99
  2.7 15.7 %all-to-all-start = ((f32[256,4,128]{2,1,0:T(4,128)}), f32[256,4,128]{2,1,0:T(4,128)S(1)}, u32[]{:S(2)}, u32[]{:S(2)}) async-start(f32[256,4,128]{2,1,0:T(4,128)} %bitcast.7), calls=%async_computation | async-start | bytes 1048576 | tf_op jit(solution)/shard_map/all_to_all | solution.py:481
  18.3 0.0 copy-start
  18.3 2.8 %copy-done = f32[2,512,4,3,128]{4,2,3,1,0:T(4,128)S(1)} copy-done((f32[2,512,4,3,128]{4,2,3,1,0:T(4,128)S(1)}, f32[2,512,4,3,128]{4,2,3,1,0:T(4,128)}, u32[]{:S(2)}) %copy-start) | copy-done | bytes 6291480
  21.1 0.0 copy-start.2
  21.1 1.0 copy-done.2
  22.2 0.0 copy-start.3
  22.2 0.9 copy-done.3
  23.1 0.0 copy-start.6
  23.1 4.0 %prepare.1 = (bf16[2,6,512,256]{3,2,1,0:T(8,128)(2,1)}, bf16[2,6,512,256]{3,2,1,0:T(8,128)(2,1)}, f32[8,128,128]{2,1,0:T(8,128)}, bf16[128,512]{1,0:T(8,128)(2,1...) custom-call(f32[2,6144,128]{2,1,0:T(8,128)S(1)} %bitcast.5, f32[2,128,512]{2,1,0:T(8,128)S(1)} %copy-done.2, ...), custom_call_target="tpu_custom_call" | custom-call | tf_op jit(solution)/shard_map/prepare/pallas_call | solution.py:145
  27.0 0.0 copy-start.1
  27.1 1.4 %collective-permute-start.2 = (f32[8,128,128]{2,1,0:T(8,128)}, f32[8,128,128]{2,1,0:T(8,128)S(1)}, u32[]{:S(2)}, u32[]{:S(2)}) collective-permute-start(f32[8,128,128]{2,1,0:T(8,128)} %get-tuple-element.26.own_ref), channel_id=1, source_target_pairs={{24,0},{0,8},{8,16},{16,24},{56,32},{32,40},{40,48},{48,56},{88,64... | collective-permute-start | bytes 1572872 | tf_op jit(solution)/shard_map/ppermute | solution.py:487
  28.4 2.5 %collective-permute-start.1 = (f32[8,128,128]{2,1,0:T(8,128)}, f32[8,128,128]{2,1,0:T(8,128)S(1)}, u32[]{:S(2)}, u32[]{:S(2)}) collective-permute-start(f32[8,128,128]{2,1,0:T(8,128)} %get-tuple-element.26.own_ref), channel_id=1, source_target_pairs={{16,0},{24,8},{0,16},{8,24},{48,32},{56,40},{32,48},{40,56},{80,64... | collective-permute-start | bytes 1572872 | tf_op jit(solution)/shard_map/ppermute | solution.py:487
  30.9 1.1 collective-permute-start
  32.0 6.2 %all-to-all-done = f32[256,4,128]{2,1,0:T(4,128)S(1)} async-done(((f32[256,4,128]{2,1,0:T(4,128)}), f32[256,4,128]{2,1,0:T(4,128)S(1)}, u32[]{:S(2)}, u32[]{:S(2)}) %all-to-all-start) | async-done | bytes 524320 | tf_op jit(solution)/shard_map/all_to_all | solution.py:481
  38.2 0.0 copy-done.6
  38.2 2.1 %near_first.1 = (f32[3,32,128]{2,1,0:T(8,128)S(1)}, f32[8,32,128]{2,1,0:T(8,128)S(1)}, bf16[3,4,64,256]{3,2,1,0:T(8,128)(2,1)S(1)}, f32[3,32,32]{2,1,0:T(8,128)S(1)}, f32[4,256]{1,0:T(4,128)S(1)}) custom-call(f32[1024,128]{1,0:T(8,128)S(1)} %bitcast.6, f32[3,512]{1,0:T(4,128)S(1)} %copy-done.6, f32[4,3,32,128]{3,2,1,0:T(8,128)S(1)} %get-tuple-element.17.mine_ref), custom_call_target="tpu_custom_call" | custom-call | tf_op jit(solution)/shard_map/near_first/pallas_call | solution.py:249
  40.3 0.0 copy-start.4
  40.3 10.0 %all_to_all.40.parts_ref = f32[8,32,128]{2,1,0:T(8,128)S(1)} all-to-all(f32[8,32,128]{2,1,0:T(8,128)S(1)} %get-tuple-element.18), channel_id=1, replica_groups=mesh['row'=32,'col'=8] {'col'}, dimensions={0} | all-to-all | bytes 262144 | tf_op jit(solution)/shard_map/all_to_all | solution.py:489
  50.3 0.2 first_solve.1
  50.5 6.9 %all_to_all.41.got_ref = f32[4,40,128]{2,1,0:T(8,128)S(1)} all-to-all(f32[4,40,128]{2,1,0:T(8,128)S(1)} %first_solve.1), channel_id=1, replica_groups={{0,8,16,24},{32,40,48,56},{64,72,80,88},{96,104,112,120},{128,136,144,1..., dimensions={0} | all-to-all | bytes 163840 | tf_op jit(solution)/shard_map/all_to_all | solution.py:474
  57.4 0.0 copy-done.4
  57.4 0.7 add.1
  58.1 5.8 %all-to-all-start.3 = ((f32[8,32,128]{2,1,0:T(8,128)}), f32[8,32,128]{2,1,0:T(8,128)S(1)}, u32[]{:S(2)}, u32[]{:S(2)}) async-start(f32[8,32,128]{2,1,0:T(8,128)} %add.1), calls=%async_computation.3 | async-start | bytes 262144 | tf_op jit(solution)/shard_map/all_to_all | solution.py:474
  63.9 0.0 copy-start.5
  63.9 0.8 copy-done.5
  64.7 4.7 %near_rest.1.rest_ref = f32[3,3,32,128]{3,2,1,0:T(8,128)S(1)} custom-call(f32[3,512]{1,0:T(4,128)S(1)} %copy-done.6, f32[4,3,32,128]{3,2,1,0:T(8,128)S(1)} %get-tuple-element.17.mine_ref, bf16[3,4,64,256]{3,2,1,0:T(8,128)(2,1)S(1)} %get-tuple-element.22.push_ref, f32[3,32,32]{2,1,0:T(8,128)S(1)} %copy-done.5, f32[4,256]{1,0:T(4,128)S(1)} %get-tuple-element.24.flags_ref), custom_call_target="tpu_custom_call" | custom-call | tf_op jit(solution)/shard_map/near_rest/pallas_call | solution.py:280
  69.4 2.2 %all-to-all-done.3.parts_ref = f32[8,32,128]{2,1,0:T(8,128)S(1)} async-done(((f32[8,32,128]{2,1,0:T(8,128)}), f32[8,32,128]{2,1,0:T(8,128)S(1)}, u32[]{:S(2)}, u32[]{:S(2)}) %all-to-all-start.3) | async-done | bytes 131104 | tf_op jit(solution)/shard_map/all_to_all | solution.py:474
  71.6 0.0 collective-permute-done.2.three_ref
  71.6 0.0 collective-permute-done.1.two_ref
  71.7 0.0 collective-permute-done.one_ref
  71.7 0.0 copy-done.1
  71.7 0.3 diagonal.1
  71.9 11.3 %all_to_all.42.parts_ref = f32[8,32,128]{2,1,0:T(8,128)S(1)} all-to-all(f32[8,32,128]{2,1,0:T(8,128)S(1)} %get-tuple-element.27), channel_id=1, replica_groups=mesh['row'=32,'col'=8] {'col'}, dimensions={0} | all-to-all | bytes 262144 | tf_op jit(solution)/shard_map/all_to_all | solution.py:495
  83.2 0.3 second_solve.1
  83.5 11.0 %all_to_all.43.parts_ref = f32[8,32,128]{2,1,0:T(8,128)S(1)} all-to-all(f32[8,32,128]{2,1,0:T(8,128)S(1)} %second_solve.1), channel_id=1, replica_groups={{0,32,64,96,128,160,192,224},{8,40,72,104,136,168,200,232},{16,48,80,11..., dimensions={0} | all-to-all | bytes 262144 | tf_op jit(solution)/shard_map/all_to_all | solution.py:474
  94.5 8.0 %all_to_all.44.got_ref = f32[4,64,128]{2,1,0:T(8,128)S(1)} all-to-all(f32[4,64,128]{2,1,0:T(8,128)S(1)} %gather.1), channel_id=1, replica_groups={{0,8,16,24},{32,40,48,56},{64,72,80,88},{96,104,112,120},{128,136,144,1..., dimensions={0} | all-to-all | bytes 262144 | tf_op jit(solution)/shard_map/all_to_all | solution.py:474
  102.5 5.1 %change.1 = f32[8,4,3,4,128]{4,3,2,1,0:T(4,128)} custom-call(f32[4,64,128]{2,1,0:T(8,128)S(1)} %all_to_all.44.got_ref, bf16[2,6,512,256]{3,2,1,0:T(8,128)(2,1)} %get-tuple-element.29.fh_hbm, bf16[2,6,512,256]{3,2,1,0:T(8,128)(2,1)} %get-tuple-element.30.fl_hbm, f32[3,32,128]{2,1,0:T(8,128)S(1)} %get-tuple-element.21.near_ref.first_ref, ...), custom_call_target="tpu_custom_call" | custom-call | tf_op jit(solution)/shard_map/change/pallas_call | solution.py:458
  107.6 7.1 %all-to-all-start.7 = ((f32[8,4,3,4,128]{4,3,2,1,0:T(4,128)}), f32[8,4,3,4,128]{4,3,2,1,0:T(4,128)S(1)}, u32[]{:S(2)}, u32[]{:S(2)}) async-start(f32[8,4,3,4,128]{4,3,2,1,0:T(4,128)} %change.1), calls=%async_computation.7 | async-start | bytes 393216 | tf_op jit(solution)/shard_map/all_to_all | solution.py:498
  114.7 0.7 answers.1
  115.3 5.2 %all-to-all-done.7 = f32[8,4,3,4,128]{4,3,2,1,0:T(4,128)S(1)} async-done(((f32[8,4,3,4,128]{4,3,2,1,0:T(4,128)}), f32[8,4,3,4,128]{4,3,2,1,0:T(4,128)S(1)}, u32[]{:S(2)}, u32[]{:S(2)}) %all-to-all-start.7) | async-done | bytes 196640 | tf_op jit(solution)/shard_map/all_to_all | solution.py:498
  120.6 0.6 reduce_sum.9
  (1 shorter events, 0.0 us)
Async XLA Ops:
  2.7 35.5 %all-to-all-start = ((f32[256,4,128]{2,1,0:T(4,128)}), f32[256,4,128]{2,1,0:T(4,128)S(1)}, u32[]{:S(2)}, u32[]{:S(2)}) async-start(f32[256,4,128]{2,1,0:T(4,128)} %bitcast.7), calls=%async_computation | async-start | bytes 1048576 | tf_op jit(solution)/shard_map/all_to_all | solution.py:481
  18.3 2.8 %copy-start = (f32[2,512,4,3,128]{4,2,3,1,0:T(4,128)S(1)}, f32[2,512,4,3,128]{4,2,3,1,0:T(4,128)}, u32[]{:S(2)}) copy-start(f32[2,512,4,3,128]{4,2,3,1,0:T(4,128)} %param.12) | copy-start | bytes 18874372
  21.1 1.0 copy-start.2
  22.2 0.9 copy-start.3
  23.1 15.1 %copy-start.6 = (f32[3,512]{1,0:T(4,128)S(1)}, f32[3,512]{1,0:T(4,128)}, u32[]{:S(2)}) copy-start(f32[3,512]{1,0:T(4,128)} %points_ref.3) | copy-start | bytes 18436
  27.0 44.6 %copy-start.1 = (f32[8,128,128]{2,1,0:T(8,128)S(1)}, f32[8,128,128]{2,1,0:T(8,128)}, u32[]{:S(2)}) copy-start(f32[8,128,128]{2,1,0:T(8,128)} %get-tuple-element.26.own_ref) | copy-start | bytes 1572868
  27.1 44.6 %collective-permute-start.2 = (f32[8,128,128]{2,1,0:T(8,128)}, f32[8,128,128]{2,1,0:T(8,128)S(1)}, u32[]{:S(2)}, u32[]{:S(2)}) collective-permute-start(f32[8,128,128]{2,1,0:T(8,128)} %get-tuple-element.26.own_ref), channel_id=1, source_target_pairs={{24,0},{0,8},{8,16},{16,24},{56,32},{32,40},{40,48},{48,56},{88,64... | collective-permute-start | bytes 1572872 | tf_op jit(solution)/shard_map/ppermute | solution.py:487
  28.4 43.2 %collective-permute-start.1 = (f32[8,128,128]{2,1,0:T(8,128)}, f32[8,128,128]{2,1,0:T(8,128)S(1)}, u32[]{:S(2)}, u32[]{:S(2)}) collective-permute-start(f32[8,128,128]{2,1,0:T(8,128)} %get-tuple-element.26.own_ref), channel_id=1, source_target_pairs={{16,0},{24,8},{0,16},{8,24},{48,32},{56,40},{32,48},{40,56},{80,64... | collective-permute-start | bytes 1572872 | tf_op jit(solution)/shard_map/ppermute | solution.py:487
  30.9 40.8 %collective-permute-start = (f32[8,128,128]{2,1,0:T(8,128)}, f32[8,128,128]{2,1,0:T(8,128)S(1)}, u32[]{:S(2)}, u32[]{:S(2)}) collective-permute-start(f32[8,128,128]{2,1,0:T(8,128)} %get-tuple-element.26.own_ref), channel_id=1, source_target_pairs={{8,0},{16,8},{24,16},{0,24},{40,32},{48,40},{56,48},{32,56},{72,64... | collective-permute-start | bytes 1572872 | tf_op jit(solution)/shard_map/ppermute | solution.py:487
  40.3 17.2 %copy-start.4 = (f32[3,32,32]{2,1,0:T(8,128)}, f32[3,32,32]{2,1,0:T(8,128)S(1)}, u32[]{:S(2)}) copy-start(f32[3,32,32]{2,1,0:T(8,128)S(1)} %get-tuple-element.23.places_ref) | copy-start | bytes 36868
  58.1 13.5 %all-to-all-start.3 = ((f32[8,32,128]{2,1,0:T(8,128)}), f32[8,32,128]{2,1,0:T(8,128)S(1)}, u32[]{:S(2)}, u32[]{:S(2)}) async-start(f32[8,32,128]{2,1,0:T(8,128)} %add.1), calls=%async_computation.3 | async-start | bytes 262144 | tf_op jit(solution)/shard_map/all_to_all | solution.py:474
  63.9 0.8 copy-start.5
  107.6 13.0 %all-to-all-start.7 = ((f32[8,4,3,4,128]{4,3,2,1,0:T(4,128)}), f32[8,4,3,4,128]{4,3,2,1,0:T(4,128)S(1)}, u32[]{:S(2)}, u32[]{:S(2)}) async-start(f32[8,4,3,4,128]{4,3,2,1,0:T(4,128)} %change.1), calls=%async_computation.7 | async-start | bytes 393216 | tf_op jit(solution)/shard_map/all_to_all | solution.py:498

commit v2 on v1

--- a/solution.py
+++ b/solution.py
@@ -1,11 +1,10 @@
-import functools
-
 import jax
 import jax.numpy as jnp
 from jax import lax
 from jax.experimental import pallas as pl
 from jax.experimental.pallas import tpu as pltpu
 from jax.sharding import PartitionSpec as P
+
 
 ROWS = 32
 COLS = 8
@@ -19,6 +18,7 @@
 RING = 4
 DEPTH = 8
 EIGHT = RHS // RING
+
 
 ON_CHIP = pl.BlockSpec(memory_space=pltpu.VMEM)
 IN_PLACE = pl.BlockSpec(memory_space=pltpu.HBM)
@@ -114,7 +114,25 @@
     )(stay(forces), stay(particles), stay(neighbours))
 
 
-def prepare_kernel(factor_ref, inverses_ref, carried_ref, fh_ref, fl_ref, lend_ref, ih_ref, il_ref, mine_ref):
+def lend_kernel(inverses_hbm, out_hbm, done):
+    copy = pltpu.make_async_copy(inverses_hbm.at[0], out_hbm, done)
+    copy.start()
+    copy.wait()
+
+
+def lend(inverses):
+    return pl.pallas_call(
+        lend_kernel,
+        out_shape=pltpu.HBM(inverses.shape[1:], jnp.float32),
+        in_specs=[IN_PLACE],
+        out_specs=IN_PLACE,
+        scratch_shapes=[pltpu.SemaphoreType.DMA],
+        name="lend",
+        compiler_params=GRANT,
+    )(stay(inverses))
+
+
+def prepare_kernel(factor_ref, inverses_ref, carried_ref, _, fh_ref, fl_ref, late_ref, mine_ref):
     for panel in range(2):
         for comp in range(COMPS):
             for block in range(BLOCKS_DEV):
@@ -127,12 +145,10 @@
                 fl_ref[panel, pair, :, lanes] = low
                 if panel == 0 and comp == 1 and block == 0:
                     for quarter in range(4):
-                        lend_ref[quarter] = value[128 * quarter : 128 * quarter + 128]
+                        late_ref[quarter] = value[128 * quarter : 128 * quarter + 128]
     for quarter in range(4):
-        lend_ref[4 + quarter] = inverses_ref[1, :, pl.ds(128 * quarter, 128)]
-    high, low = halves(inverses_ref[0])
-    ih_ref[...] = high
-    il_ref[...] = low
+        lanes = pl.ds(128 * quarter, 128)
+        late_ref[4 + quarter] = inverses_ref[1, :, lanes]
     owner = lax.broadcasted_iota(jnp.int32, (RHS, 128), 0) // SHARE
     own = owner == jnp.full((RHS, 128), lax.axis_index("col"), jnp.int32)
     for block in range(BLOCKS_DEV):
@@ -140,7 +156,7 @@
             mine_ref[block, comp] = jnp.where(own, carried_ref[block, comp], 0.0)
 
 
-def prepare(factor_rows, inverses, carried):
+def prepare(factor_rows, inverses, carried, early):
     panels = (2, 2 * COMPS, COLUMNS, 256)
     return pl.pallas_call(
         prepare_kernel,
@@ -148,15 +164,13 @@
             pltpu.HBM(panels, jnp.bfloat16),
             pltpu.HBM(panels, jnp.bfloat16),
             pltpu.HBM((8, 128, 128), jnp.float32),
-            kept((128, COLUMNS), jnp.bfloat16),
-            kept((128, COLUMNS), jnp.bfloat16),
             kept(carried.shape),
         ),
-        in_specs=[ON_CHIP] * 3,
-        out_specs=(ON_CHIP,) * 6,
+        in_specs=[ON_CHIP] * 3 + [IN_PLACE],
+        out_specs=(ON_CHIP,) * 4,
         name="prepare",
         compiler_params=GRANT,
-    )(factor_rows, inverses, carried)
+    )(factor_rows, inverses, carried, stay(early))
 
 
 def fill(places_ref, source):
@@ -240,9 +254,10 @@
     for comp in range(COMPS):
         value = totals[comp] + mine_ref[0, comp]
         out_ref[comp] = value
-        if comp == 0:
-            for part in range(COLS):
-                spread_ref[part] = value
+        if comp < 2:
+            for part in range(RING * COLS):
+                y = part // COLS
+                spread_ref[part, pl.ds(EIGHT * comp, EIGHT), :] = value[EIGHT * y : EIGHT * y + EIGHT]
 
 
 def near_first(got, points, mine):
@@ -250,10 +265,10 @@
         near_first_kernel,
         out_shape=(
             kept((COMPS, RHS, 128)),
-            kept((COLS, RHS, 128)),
-            kept((COMPS, 4, 64, 256), jnp.bfloat16),
-            kept((COMPS, SLICE, ROWS)),
-            kept((BLOCKS_DEV, 256)),
+            pltpu.HBM((RING * COLS, 2 * EIGHT, 128), jnp.float32),
+            pltpu.HBM((COMPS, 4, 64, 256), jnp.bfloat16),
+            pltpu.HBM((COMPS, SLICE, ROWS), jnp.float32),
+            pltpu.HBM((BLOCKS_DEV, 256), jnp.float32),
         ),
         in_specs=[ON_CHIP] * 3,
         out_specs=(ON_CHIP,) * 5,
@@ -286,7 +301,7 @@
         + [pltpu.VMEM((2, 6, 256, 256), jnp.bfloat16)] * 2,
         name="near_rest",
         compiler_params=GRANT,
-    )(points, keep(mine), keep(push), keep(places), keep(flags))
+    )(points, keep(mine), stay(push), stay(places), stay(flags))
 
 
 def total(parts_ref):
@@ -296,123 +311,106 @@
     return value
 
 
-def first_solve_kernel(parts_ref, ih_ref, il_ref, near_ref, out_ref):
-    value = product(total(parts_ref), ih_ref[...], il_ref[...])
+def first_solve_kernel(parts_ref, own_ref, one_ref, two_ref, three_ref, out_ref, base_ref):
+    ring_at = lax.axis_index("row") % RING
     for y in range(RING):
-        sides = slice(EIGHT * y, EIGHT * y + EIGHT)
-        for quarter in range(4):
-            out_ref[y, pl.ds(EIGHT * quarter, EIGHT), :] = value[sides, 128 * quarter : 128 * quarter + 128]
-        out_ref[y, pl.ds(32, EIGHT), :] = near_ref[1, pl.ds(EIGHT * y, EIGHT), :]
-
-
-def first_solve(parts, ih, il, near):
-    return pl.pallas_call(
-        first_solve_kernel,
-        out_shape=kept((RING, 40, 128)),
-        in_specs=[ON_CHIP] * 4,
-        out_specs=ON_CHIP,
-        name="first_solve",
-        compiler_params=GRANT,
-    )(keep(parts), keep(ih), keep(il), keep(near))
-
-
-def add_kernel(got_ref, out_ref):
-    value = total(got_ref)[0:32]
-    for part in range(DEPTH):
-        out_ref[part] = value
-
-
-def add(got):
-    return pl.pallas_call(
-        add_kernel,
-        out_shape=kept((DEPTH, 32, 128)),
-        in_specs=[ON_CHIP],
-        out_specs=ON_CHIP,
-        name="add",
-        compiler_params=GRANT,
-    )(keep(got))
-
-
-def wide(value):
-    return jnp.concatenate([value[EIGHT * q : EIGHT * q + EIGHT] for q in range(4)], axis=1)
-
-
-def diagonal_kernel(parts_ref, got_ref, own_ref, one_ref, two_ref, three_ref, answer_ref, out_ref):
-    value = total(parts_ref)
-    answer_ref[...] = value
-    answer = wide(value)
-    y = lax.axis_index("row") % RING
-    for step, tiles in enumerate((own_ref, one_ref, two_ref, three_ref)):
-        columns = jnp.concatenate([tiles[quarter] for quarter in range(4)], axis=0)
-        base = got_ref[(y + step) % RING, pl.ds(32, EIGHT), :]
-        value = base - product(answer, *halves(columns))
-        for part in range(COLS):
-            out_ref[part, pl.ds(EIGHT * step, EIGHT), :] = value
-
-
-def diagonal(parts, got, tiles):
-    return pl.pallas_call(
-        diagonal_kernel,
-        out_shape=(kept((32, 128)), kept((COLS, 32, 128))),
-        in_specs=[ON_CHIP] * 6,
-        out_specs=(ON_CHIP,) * 2,
-        name="diagonal",
-        compiler_params=GRANT,
-    )(keep(parts), keep(got), *[keep(tile) for tile in tiles])
-
-
-def second_solve_kernel(parts_ref, own_ref, one_ref, two_ref, three_ref, out_ref):
-    diag = total(parts_ref)
+        value = parts_ref[COLS * y]
+        for part in range(1, COLS):
+            value = value + parts_ref[COLS * y + part]
+        base_ref[y] = value
     value = None
     for step, tiles in enumerate((own_ref, one_ref, two_ref, three_ref)):
-        inverse = jnp.concatenate([tiles[4 + quarter] for quarter in range(4)], axis=1)
-        add = product(diag[EIGHT * step : EIGHT * step + EIGHT], *halves(inverse))
+        diag = base_ref[(ring_at + step) % RING, pl.ds(0, EIGHT), :]
+        add = product(diag, *halves(tiles[...]))
         value = add if value is None else value + add
     for part in range(DEPTH):
         for quarter in range(4):
             out_ref[part, pl.ds(EIGHT * quarter, EIGHT), :] = value[:, 128 * quarter : 128 * quarter + 128]
 
 
-def second_solve(parts, tiles):
+def first_solve(parts, tiles):
+    return pl.pallas_call(
+        first_solve_kernel,
+        out_shape=(kept((DEPTH, 32, 128)), kept((RING, 2 * EIGHT, 128))),
+        in_specs=[ON_CHIP] * 5,
+        out_specs=(ON_CHIP,) * 2,
+        name="first_solve",
+        compiler_params=GRANT,
+    )(keep(parts), *[keep(tile) for tile in tiles])
+
+
+def wide(value):
+    return jnp.concatenate([value[EIGHT * q : EIGHT * q + EIGHT] for q in range(4)], axis=1)
+
+
+def diagonal_kernel(parts_ref, own_ref, one_ref, two_ref, three_ref, answer_ref, out_ref):
+    value = total(parts_ref)
+    answer_ref[...] = value
+    answer = wide(value)
+    for step, tiles in enumerate((own_ref, one_ref, two_ref, three_ref)):
+        columns = jnp.concatenate([tiles[quarter] for quarter in range(4)], axis=0)
+        value = product(answer, *halves(columns))
+        for part in range(COLS):
+            out_ref[part, pl.ds(EIGHT * step, EIGHT), :] = value
+
+
+def diagonal(parts, tiles):
+    return pl.pallas_call(
+        diagonal_kernel,
+        out_shape=(kept((32, 128)), kept((COLS, 32, 128))),
+        in_specs=[ON_CHIP] * 5,
+        out_specs=(ON_CHIP,) * 2,
+        name="diagonal",
+        compiler_params=GRANT,
+    )(keep(parts), *[keep(tile) for tile in tiles])
+
+
+def second_solve_kernel(parts_ref, base_ref, answer_ref, own_ref, one_ref, two_ref, three_ref, out_ref):
+    row = lax.axis_index("row")
+    change = total(parts_ref)
+    value = None
+    for step, tiles in enumerate((own_ref, one_ref, two_ref, three_ref)):
+        inverse = jnp.concatenate([tiles[4 + quarter] for quarter in range(4)], axis=1)
+        base = base_ref[(row % RING + step) % RING, pl.ds(EIGHT, EIGHT), :]
+        add = product(base - change[EIGHT * step : EIGHT * step + EIGHT], *halves(inverse))
+        value = add if value is None else value + add
+    tail = [answer_ref[pl.ds(EIGHT * quarter + row // RING, 1), :] for quarter in range(4)]
+    tail = jnp.concatenate([*tail, jnp.zeros((4, 128), jnp.float32)], axis=0)
+    for part in range(ROWS):
+        for quarter in range(4):
+            out_ref[part, pl.ds(EIGHT * quarter, EIGHT), :] = value[:, 128 * quarter : 128 * quarter + 128]
+        out_ref[part, pl.ds(32, EIGHT), :] = tail
+
+
+def second_solve(parts, base, answer, tiles):
     return pl.pallas_call(
         second_solve_kernel,
-        out_shape=kept((DEPTH, 32, 128)),
-        in_specs=[ON_CHIP] * 5,
+        out_shape=kept((ROWS, 40, 128)),
+        in_specs=[ON_CHIP] * 7,
         out_specs=ON_CHIP,
         name="second_solve",
         compiler_params=GRANT,
-    )(keep(parts), *[keep(tile) for tile in tiles])
-
-
-def gather_kernel(parts_ref, first_ref, out_ref):
-    second = total(parts_ref)
+    )(keep(parts), keep(base), keep(answer), *[keep(tile) for tile in tiles])
+
+
+def whole(got_ref):
+    first, second = [], []
+    sums = []
     for y in range(RING):
-        out_ref[y, 0:32] = first_ref[...]
-        out_ref[y, 32:64] = second
-
-
-def gather(parts, first):
-    return pl.pallas_call(
-        gather_kernel,
-        out_shape=kept((RING, 64, 128)),
-        in_specs=[ON_CHIP] * 2,
-        out_specs=ON_CHIP,
-        name="gather",
-        compiler_params=GRANT,
-    )(keep(parts), keep(first))
-
-
-def whole(got_ref, panel):
-    columns = []
+        value = got_ref[pl.ds(40 * y, 32), :]
+        for z in range(1, DEPTH):
+            value = value + got_ref[pl.ds(40 * (RING * z + y), 32), :]
+        sums.append(value)
     for quarter in range(4):
-        rows = pl.ds(32 * panel + EIGHT * quarter, EIGHT)
-        columns.append(jnp.concatenate([got_ref[y, rows, :] for y in range(RING)], axis=0))
-    return jnp.concatenate(columns, axis=1)
+        lines = [got_ref[pl.ds(40 * y + 32 + quarter, DEPTH, stride=40 * RING), :] for y in range(RING)]
+        first.append(jnp.concatenate(lines, axis=0))
+        lines = [value[EIGHT * quarter : EIGHT * quarter + EIGHT] for value in sums]
+        second.append(jnp.concatenate(lines, axis=0))
+    return jnp.concatenate(first, axis=1), jnp.concatenate(second, axis=1)
 
 
 def answers_kernel(got_ref, out_ref):
-    for panel in range(2):
-        out_ref[panel] = whole(got_ref, panel)
+    out_ref[0], out_ref[1] = whole(got_ref)
 
 
 def answers(got):
@@ -435,7 +433,7 @@
         copies.append(pltpu.make_async_copy(fl_hbm.at[panel, pair], low.at[at], read.at[count + at]))
     for copy in copies:
         copy.start()
-    sides = [whole(got_ref, panel) for panel in range(2)]
+    sides = whole(got_ref)
     for comp in range(COMPS):
         for pair in range(2):
             moved = []
@@ -470,31 +468,34 @@
     )(keep(got), stay(fh), stay(fl), keep(first), keep(rest))
 
 
-def along(array, groups):
-    return lax.all_to_all(array, "row", 0, 0, axis_index_groups=groups, tiled=True)
-
-
 def body(obstacles, particles, forces, neighbours, carried, factor, inverses):
-    ring = [[RING * z + y for y in range(RING)] for z in range(DEPTH)]
+    everyone = ("row", "col")
+    plane = [[32 * z + at for at in range(RING * COLS)] for z in range(DEPTH)]
     line = [[RING * z + y for z in range(DEPTH)] for y in range(RING)]
     sent = payload(forces, particles, neighbours).reshape(ROWS * COLS, SHARE, 128)
-    got = lax.all_to_all(sent, ("row", "col"), 0, 0, tiled=True).reshape(ROWS * RHS, 128)
+    got = lax.all_to_all(sent, everyone, 0, 0, tiled=True).reshape(ROWS * RHS, 128)
     rows = factor.transpose(0, 1, 3, 2, 4).reshape(2, COLUMNS * COMPS * BLOCKS_DEV, 128)
-    fh, fl, lend, ih, il, mine = prepare(rows, inverses, carried)
-    tiles = [lend]
-    for step in range(1, RING):
-        pairs = [(RING * z + (y + step) % RING, RING * z + y) for z in range(DEPTH) for y in range(RING)]
-        tiles.append(lax.ppermute(lend, "row", pairs))
+    early = lend(inverses)
+    fh, fl, late, mine = prepare(rows, inverses, carried, early)
+    tiles = []
+    for lent in (early, late):
+        shared = [lent]
+        for step in range(1, RING):
+            pairs = [
+                (RING * z + (y + step) % RING, RING * z + y) for z in range(DEPTH) for y in range(RING)
+            ]
+            shared.append(lax.ppermute(lent, "row", pairs))
+        tiles.append(shared)
     near0, spread, push, places, flags = near_first(got, obstacles, mine)
+    parts = lax.all_to_all(stay(spread), everyone, 0, 0, axis_index_groups=plane, tiled=True)
+    rest = near_rest(obstacles, mine, push, places, flags)
+    parts, rest = lax.optimization_barrier((parts, rest))
+    spread, base = first_solve(parts, tiles[0])
+    parts = lax.all_to_all(spread, "row", 0, 0, axis_index_groups=line, tiled=True)
+    first, spread = diagonal(parts, tiles[1])
     parts = lax.all_to_all(spread, "col", 0, 0, tiled=True)
-    rest = near_rest(obstacles, mine, push, places, flags)
-    shares = along(first_solve(parts, ih, il, near0), ring)
-    parts = along(add(shares), line)
-    parts, rest = lax.optimization_barrier((parts, rest))
-    first, spread = diagonal(parts, shares, tiles)
-    parts = lax.all_to_all(spread, "col", 0, 0, tiled=True)
-    parts = along(second_solve(parts, tiles), line)
-    shares = along(gather(parts, first), ring)
+    spread = second_solve(parts, base, first, tiles[1])
+    shares = lax.all_to_all(spread, "row", 0, 0, tiled=True).reshape(ROWS * 40, 128)
     back = lax.all_to_all(change(shares, fh, fl, near0, rest), "col", 0, 0, tiled=True)
     return (answers(shares), jnp.sum(back, axis=0))
 

time: 122 us -> 149 us (1.22)
  waiting for transfers between devices: 13.7 us -> 31.6 us
  blocking collectives: 47.2 us -> 34.1 us
  Pallas kernels: 19.9 us -> 31.8 us
  starting transfers between devices: 33.5 us -> 44.3 us
    all_to_all x2 -> x3, waiting for transfers between devices: 8.47 us -> 26.5 us  [the longest x1 18.6 us: body(): lax.all_to_all(stay(spread), everyone, 0, 0, axis_index_groups=plane, til...]
    pallas_call x5 -> x4, Pallas kernels: 3.16 us -> 14.1 us  [the longest x1 9.05 us: lend(): pl.pallas_call(lend_kernel, out_shape=pltpu.HBM(inverses.shape[1:], jnp.f...]
    all_to_all x2 -> x1, blocking collectives: 21.3 us -> 11.5 us  [body(): parts = lax.all_to_all(spread, 'col', 0, 0, tiled=True)]
    all_to_all x2 -> x3, starting transfers between devices: 21.4 us -> 30.7 us  [the longest x1 15.7 us: body(): lax.all_to_all(sent, everyone, 0, 0, tiled=True).reshape(ROWS * RHS, 128)]
    all_to_all x3 -> x1, blocking collectives: 25.9 us -> 22.6 us  [body(): lax.all_to_all(spread, 'row', 0, 0, tiled=True).reshape(ROWS * 40, 128)]
    ppermute x3 -> x6, starting transfers between devices: 4.93 us -> 7.8 us  [body(): shared.append(lax.ppermute(lent, 'row', pairs))]
    unnamed x14 -> x12, local copies, waits for them, and re-layouts: 5.55 us -> 4.76 us
  transfers between devices with their start and end apart: 6 -> 10, of which waited for: 3 -> 3; matrix products, arithmetic and copies ran while one was open for 0% -> 0% of each run, Pallas kernels for 10% -> 16%
where the time goes in v2:
time: 149 us; the launch traced here: 148 us
  starting transfers between devices  44.3 us (30%)
  blocking collectives  34.1 us (23%)
  Pallas kernels  31.8 us (21%)
  waiting for transfers between devices  31.6 us (21%)
  local copies, waits for them, and re-layouts  4.76 us (3%)
    all_to_all x1, blocking collectives, body(): lax.all_to_all(spread, 'row', 0, 0, tiled=True).reshape(ROWS * 40, 128)  22.6 us
    all_to_all x1, waiting for transfers between devices, body(): lax.all_to_all(stay(spread), everyone, 0, 0, axis_index_groups=plane, til...  18.6 us
    all_to_all x1, starting transfers between devices, body(): lax.all_to_all(sent, everyone, 0, 0, tiled=True).reshape(ROWS * RHS, 128)  15.7 us
    all_to_all x1, blocking collectives, body(): parts = lax.all_to_all(spread, 'col', 0, 0, tiled=True)  11.5 us
    pallas_call x1, Pallas kernels, lend(): pl.pallas_call(lend_kernel, out_shape=pltpu.HBM(inverses.shape[1:], jnp.f...  9.05 us
    all_to_all x1, waiting for transfers between devices, body(): lax.all_to_all(spread, 'row', 0, 0, axis_index_groups=line, tiled=True)  7.83 us
    ppermute x6, starting transfers between devices, body(): shared.append(lax.ppermute(lent, 'row', pairs))  7.8 us
    all_to_all x1, starting transfers between devices, body(): lax.all_to_all(stay(spread), everyone, 0, 0, axis_index_groups=plane, til...  7.64 us
  transfers between devices with their start and end apart: 10, of which 3 were waited for; matrix products, arithmetic and copies ran while one was open for 0% of the time, Pallas kernels for 16%

profile of v2, /device:TPU:1, one launch (start us, length us, event | category | flops | bytes accessed | tf_op | source)
XLA Modules:
  0.0 148.0 jit_solution(7568821175625418078)
XLA Ops:
  0.6 2.0 %payload.1 = f32[32,8,4,128]{3,2,1,0:T(4,128)} custom-call(f32[3,32,256]{2,1,0:T(8,128)} %forces_hbm.1, f32[3,256]{1,0:T(4,128)} %particles_hbm.1, s32[2,4]{1,0:T(2,128)} %neighbours_hbm.1), custom_call_target="tpu_custom_call" | custom-call | tf_op jit(solution)/shard_map/payload/pallas_call | solution.py:99
  2.7 15.7 %all-to-all-start = ((f32[256,4,128]{2,1,0:T(4,128)}), f32[256,4,128]{2,1,0:T(4,128)S(1)}, u32[]{:S(2)}, u32[]{:S(2)}) async-start(f32[256,4,128]{2,1,0:T(4,128)} %bitcast.10), calls=%async_computation | async-start | bytes 1048576 | tf_op jit(solution)/shard_map/all_to_all | solution.py:476
  18.3 9.1 %lend.1._.own_ref = f32[128,512]{1,0:T(8,128)} custom-call(f32[2,128,512]{2,1,0:T(8,128)} %inverses_ref.1), custom_call_target="tpu_custom_call" | custom-call | tf_op jit(solution)/shard_map/lend/pallas_call | solution.py:124
  27.4 1.4 collective-permute-start.2
  28.8 0.0 copy-start
  28.8 2.8 %copy-done = f32[2,512,4,3,128]{4,2,3,1,0:T(4,128)S(1)} copy-done((f32[2,512,4,3,128]{4,2,3,1,0:T(4,128)S(1)}, f32[2,512,4,3,128]{4,2,3,1,0:T(4,128)}, u32[]{:S(2)}) %copy-start) | copy-done | bytes 6291480
  31.6 0.0 copy-start.2
  31.6 1.0 copy-done.2
  32.7 0.0 copy-start.4
  32.7 0.9 copy-done.4
  33.6 0.0 copy-start.1
  33.6 0.0 copy-start.5
  33.6 4.0 %prepare.1 = (bf16[2,6,512,256]{3,2,1,0:T(8,128)(2,1)}, bf16[2,6,512,256]{3,2,1,0:T(8,128)(2,1)}, f32[8,128,128]{2,1,0:T(8,128)}, f32[4,3,32,128]{3,2,1,0:T(8,128)S(1)}) custom-call(f32[2,6144,128]{2,1,0:T(8,128)S(1)} %bitcast.6, f32[2,128,512]{2,1,0:T(8,128)S(1)} %copy-done.2, f32[4,3,32,128]{3,2,1,0:T(8,128)S(1)} %copy-done.4, f32[128,512]{1,0:T(8,128)} %lend.1._.own_ref), custom_call_target="tpu_custom_call" | custom-call | tf_op jit(solution)/shard_map/prepare/pallas_call | solution.py:161
  37.5 0.0 copy-start.3
  37.5 1.2 collective-permute-start.5
  38.7 1.3 collective-permute-start.4
  40.0 2.0 %collective-permute-start.3 = (f32[8,128,128]{2,1,0:T(8,128)}, f32[8,128,128]{2,1,0:T(8,128)S(1)}, u32[]{:S(2)}, u32[]{:S(2)}) collective-permute-start(f32[8,128,128]{2,1,0:T(8,128)} %get-tuple-element.24.own_ref), channel_id=1, source_target_pairs={{8,0},{16,8},{24,16},{0,24},{40,32},{48,40},{56,48},{32,56},{72,64... | collective-permute-start | bytes 1572872 | tf_op jit(solution)/shard_map/ppermute | solution.py:487
  42.1 0.0 copy-done.1
  42.1 0.5 collective-permute-start.1
  42.6 0.0 collective-permute-done.2.three_ref
  42.6 1.3 collective-permute-start
  43.9 0.0 all-to-all-done
  43.9 0.0 copy-done.5
  43.9 2.8 %near_first.1 = (f32[3,32,128]{2,1,0:T(8,128)S(1)}, f32[32,16,128]{2,1,0:T(8,128)}, bf16[3,4,64,256]{3,2,1,0:T(8,128)(2,1)}, f32[3,32,32]{2,1,0:T(8,128)}, f32[4,256]{1,0:T(4,128)}) custom-call(f32[1024,128]{1,0:T(8,128)S(1)} %bitcast.9, f32[3,512]{1,0:T(4,128)S(1)} %copy-done.5, f32[4,3,32,128]{3,2,1,0:T(8,128)S(1)} %get-tuple-element.17.mine_ref), custom_call_target="tpu_custom_call" | custom-call | tf_op jit(solution)/shard_map/near_first/pallas_call | solution.py:264
  46.7 7.6 %all-to-all-start.1 = ((f32[32,16,128]{2,1,0:T(8,128)}), f32[32,16,128]{2,1,0:T(8,128)S(1)}, u32[]{:S(2)}, u32[]{:S(2)}) async-start(f32[32,16,128]{2,1,0:T(8,128)} %get-tuple-element.18), calls=%async_computation.1 | async-start | bytes 524288 | tf_op jit(solution)/shard_map/all_to_all | solution.py:490
  54.3 5.6 %near_rest.1.rest_ref = f32[3,3,32,128]{3,2,1,0:T(8,128)S(1)} custom-call(f32[3,512]{1,0:T(4,128)S(1)} %copy-done.5, f32[4,3,32,128]{3,2,1,0:T(8,128)S(1)} %get-tuple-element.17.mine_ref, bf16[3,4,64,256]{3,2,1,0:T(8,128)(2,1)} %get-tuple-element.19.push_ref, f32[3,32,32]{2,1,0:T(8,128)} %get-tuple-element.20.places_ref, f32[4,256]{1,0:T(4,128)} %get-tuple-element.21.flags_ref), custom_call_target="tpu_custom_call" | custom-call | tf_op jit(solution)/shard_map/near_rest/pallas_call | solution.py:295
  60.0 18.6 %all-to-all-done.1.parts_ref = f32[32,16,128]{2,1,0:T(8,128)S(1)} async-done(((f32[32,16,128]{2,1,0:T(8,128)}), f32[32,16,128]{2,1,0:T(8,128)S(1)}, u32[]{:S(2)}, u32[]{:S(2)}) %all-to-all-start.1) | async-done | bytes 262176 | tf_op jit(solution)/shard_map/all_to_all | solution.py:490
  78.6 0.0 collective-permute-done.1.two_ref
  78.6 0.0 collective-permute-done.one_ref
  78.6 2.0 %first_solve.1 = (f32[8,32,128]{2,1,0:T(8,128)}, f32[4,16,128]{2,1,0:T(8,128)S(1)}) custom-call(f32[32,16,128]{2,1,0:T(8,128)S(1)} %all-to-all-done.1.parts_ref, f32[128,512]{1,0:T(8,128)S(1)} %copy-done.1, f32[128,512]{1,0:T(8,128)} %collective-permute-done.one_ref, f32[128,512]{1,0:T(8,128)} %collective-permute-done.1.two_ref, ...), custom_call_target="tpu_custom_call" | custom-call | tf_op jit(solution)/shard_map/first_solve/pallas_call | solution.py:332
  80.6 7.4 %all-to-all-start.2 = ((f32[8,32,128]{2,1,0:T(8,128)}), f32[8,32,128]{2,1,0:T(8,128)S(1)}, u32[]{:S(2)}, u32[]{:S(2)}) async-start(f32[8,32,128]{2,1,0:T(8,128)} %get-tuple-element.23), calls=%async_computation.2 | async-start | bytes 262144 | tf_op jit(solution)/shard_map/all_to_all | solution.py:494
  88.0 0.0 collective-permute-done.5.three_ref
  88.0 0.0 collective-permute-done.4.two_ref
  88.0 0.0 collective-permute-done.3.one_ref
  88.0 7.8 %all-to-all-done.2.parts_ref = f32[8,32,128]{2,1,0:T(8,128)S(1)} async-done(((f32[8,32,128]{2,1,0:T(8,128)}), f32[8,32,128]{2,1,0:T(8,128)S(1)}, u32[]{:S(2)}, u32[]{:S(2)}) %all-to-all-start.2) | async-done | bytes 131104 | tf_op jit(solution)/shard_map/all_to_all | solution.py:494
  95.8 0.0 copy-done.3
  95.8 0.3 diagonal.1
  96.1 11.5 %all_to_all.30.parts_ref = f32[8,32,128]{2,1,0:T(8,128)S(1)} all-to-all(f32[8,32,128]{2,1,0:T(8,128)S(1)} %get-tuple-element.25), channel_id=1, replica_groups=mesh['row'=32,'col'=8] {'col'}, dimensions={0} | all-to-all | bytes 262144 | tf_op jit(solution)/shard_map/all_to_all | solution.py:496
  107.6 0.3 second_solve.1
  107.9 22.6 %all_to_all.31 = f32[32,40,128]{2,1,0:T(8,128)S(1)} all-to-all(f32[32,40,128]{2,1,0:T(8,128)S(1)} %second_solve.1), channel_id=1, replica_groups=mesh['row'=32,'col'=8] {'row'}, dimensions={0} | all-to-all | bytes 1310720 | tf_op jit(solution)/shard_map/all_to_all | solution.py:498
  130.5 5.1 %change.1 = f32[8,4,3,4,128]{4,3,2,1,0:T(4,128)} custom-call(f32[1280,128]{1,0:T(8,128)S(1)} %bitcast.7, bf16[2,6,512,256]{3,2,1,0:T(8,128)(2,1)} %get-tuple-element.28.fh_hbm, bf16[2,6,512,256]{3,2,1,0:T(8,128)(2,1)} %get-tuple-element.29.fl_hbm, f32[3,32,128]{2,1,0:T(8,128)S(1)} %get-tuple-element.30.first_ref, f32[3,3,32,128]{3,2,1,0:T(8,128)S(1)} %near_rest.1.rest_ref), custom_call_target="tpu_custom_call" | custom-call | tf_op jit(solution)/shard_map/change/pallas_call | solution.py:456
  135.6 5.9 %all-to-all-start.5 = ((f32[8,4,3,4,128]{4,3,2,1,0:T(4,128)}), f32[8,4,3,4,128]{4,3,2,1,0:T(4,128)S(1)}, u32[]{:S(2)}, u32[]{:S(2)}) async-start(f32[8,4,3,4,128]{4,3,2,1,0:T(4,128)} %change.1), calls=%async_computation.5 | async-start | bytes 393216 | tf_op jit(solution)/shard_map/all_to_all | solution.py:499
  141.4 0.7 answers.1
  142.1 5.2 %all-to-all-done.5 = f32[8,4,3,4,128]{4,3,2,1,0:T(4,128)S(1)} async-done(((f32[8,4,3,4,128]{4,3,2,1,0:T(4,128)}), f32[8,4,3,4,128]{4,3,2,1,0:T(4,128)S(1)}, u32[]{:S(2)}, u32[]{:S(2)}) %all-to-all-start.5) | async-done | bytes 196640 | tf_op jit(solution)/shard_map/all_to_all | solution.py:499
  147.3 0.6 reduce_sum.9
Async XLA Ops:
  2.7 41.2 %all-to-all-start = ((f32[256,4,128]{2,1,0:T(4,128)}), f32[256,4,128]{2,1,0:T(4,128)S(1)}, u32[]{:S(2)}, u32[]{:S(2)}) async-start(f32[256,4,128]{2,1,0:T(4,128)} %bitcast.10), calls=%async_computation | async-start | bytes 1048576 | tf_op jit(solution)/shard_map/all_to_all | solution.py:476
  27.4 15.2 %collective-permute-start.2 = (f32[128,512]{1,0:T(8,128)}, f32[128,512]{1,0:T(8,128)S(1)}, u32[]{:S(2)}, u32[]{:S(2)}) collective-permute-start(f32[128,512]{1,0:T(8,128)} %lend.1._.own_ref), channel_id=1, source_target_pairs={{24,0},{0,8},{8,16},{16,24},{56,32},{32,40},{40,48},{48,56},{88,64... | collective-permute-start | bytes 786440 | tf_op jit(solution)/shard_map/ppermute | solution.py:487
  28.8 2.8 %copy-start = (f32[2,512,4,3,128]{4,2,3,1,0:T(4,128)S(1)}, f32[2,512,4,3,128]{4,2,3,1,0:T(4,128)}, u32[]{:S(2)}) copy-start(f32[2,512,4,3,128]{4,2,3,1,0:T(4,128)} %param.12) | copy-start | bytes 18874372
  31.6 1.0 copy-start.2
  32.7 0.9 copy-start.4
  33.6 8.5 %copy-start.1 = (f32[128,512]{1,0:T(8,128)S(1)}, f32[128,512]{1,0:T(8,128)}, u32[]{:S(2)}) copy-start(f32[128,512]{1,0:T(8,128)} %lend.1._.own_ref) | copy-start | bytes 786436
  33.6 10.3 %copy-start.5 = (f32[3,512]{1,0:T(4,128)S(1)}, f32[3,512]{1,0:T(4,128)}, u32[]{:S(2)}) copy-start(f32[3,512]{1,0:T(4,128)} %points_ref.3) | copy-start | bytes 18436
  37.5 58.3 %copy-start.3 = (f32[8,128,128]{2,1,0:T(8,128)S(1)}, f32[8,128,128]{2,1,0:T(8,128)}, u32[]{:S(2)}) copy-start(f32[8,128,128]{2,1,0:T(8,128)} %get-tuple-element.24.own_ref) | copy-start | bytes 1572868
  37.5 50.4 %collective-permute-start.5 = (f32[8,128,128]{2,1,0:T(8,128)}, f32[8,128,128]{2,1,0:T(8,128)S(1)}, u32[]{:S(2)}, u32[]{:S(2)}) collective-permute-start(f32[8,128,128]{2,1,0:T(8,128)} %get-tuple-element.24.own_ref), channel_id=1, source_target_pairs={{24,0},{0,8},{8,16},{16,24},{56,32},{32,40},{40,48},{48,56},{88,64... | collective-permute-start | bytes 1572872 | tf_op jit(solution)/shard_map/ppermute | solution.py:487
  38.7 49.2 %collective-permute-start.4 = (f32[8,128,128]{2,1,0:T(8,128)}, f32[8,128,128]{2,1,0:T(8,128)S(1)}, u32[]{:S(2)}, u32[]{:S(2)}) collective-permute-start(f32[8,128,128]{2,1,0:T(8,128)} %get-tuple-element.24.own_ref), channel_id=1, source_target_pairs={{16,0},{24,8},{0,16},{8,24},{48,32},{56,40},{32,48},{40,56},{80,64... | collective-permute-start | bytes 1572872 | tf_op jit(solution)/shard_map/ppermute | solution.py:487
  40.0 47.9 %collective-permute-start.3 = (f32[8,128,128]{2,1,0:T(8,128)}, f32[8,128,128]{2,1,0:T(8,128)S(1)}, u32[]{:S(2)}, u32[]{:S(2)}) collective-permute-start(f32[8,128,128]{2,1,0:T(8,128)} %get-tuple-element.24.own_ref), channel_id=1, source_target_pairs={{8,0},{16,8},{24,16},{0,24},{40,32},{48,40},{56,48},{32,56},{72,64... | collective-permute-start | bytes 1572872 | tf_op jit(solution)/shard_map/ppermute | solution.py:487
  42.1 36.5 %collective-permute-start.1 = (f32[128,512]{1,0:T(8,128)S(1)}, f32[128,512]{1,0:T(8,128)}, u32[]{:S(2)}, u32[]{:S(2)}) collective-permute-start(f32[128,512]{1,0:T(8,128)S(1)} %copy-done.1), channel_id=1, source_target_pairs={{16,0},{24,8},{0,16},{8,24},{48,32},{56,40},{32,48},{40,56},{80,64... | collective-permute-start | bytes 786440 | tf_op jit(solution)/shard_map/ppermute | solution.py:487
  42.6 36.0 %collective-permute-start = (f32[128,512]{1,0:T(8,128)S(1)}, f32[128,512]{1,0:T(8,128)}, u32[]{:S(2)}, u32[]{:S(2)}) collective-permute-start(f32[128,512]{1,0:T(8,128)S(1)} %copy-done.1), channel_id=1, source_target_pairs={{8,0},{16,8},{24,16},{0,24},{40,32},{48,40},{56,48},{32,56},{72,64... | collective-permute-start | bytes 786440 | tf_op jit(solution)/shard_map/ppermute | solution.py:487
  46.7 31.9 %all-to-all-start.1 = ((f32[32,16,128]{2,1,0:T(8,128)}), f32[32,16,128]{2,1,0:T(8,128)S(1)}, u32[]{:S(2)}, u32[]{:S(2)}) async-start(f32[32,16,128]{2,1,0:T(8,128)} %get-tuple-element.18), calls=%async_computation.1 | async-start | bytes 524288 | tf_op jit(solution)/shard_map/all_to_all | solution.py:490
  80.6 15.2 %all-to-all-start.2 = ((f32[8,32,128]{2,1,0:T(8,128)}), f32[8,32,128]{2,1,0:T(8,128)S(1)}, u32[]{:S(2)}, u32[]{:S(2)}) async-start(f32[8,32,128]{2,1,0:T(8,128)} %get-tuple-element.23), calls=%async_computation.2 | async-start | bytes 262144 | tf_op jit(solution)/shard_map/all_to_all | solution.py:494
  135.6 11.7 %all-to-all-start.5 = ((f32[8,4,3,4,128]{4,3,2,1,0:T(4,128)}), f32[8,4,3,4,128]{4,3,2,1,0:T(4,128)S(1)}, u32[]{:S(2)}, u32[]{:S(2)}) async-start(f32[8,4,3,4,128]{4,3,2,1,0:T(4,128)} %change.1), calls=%async_computation.5 | async-start | bytes 393216 | tf_op jit(solution)/shard_map/all_to_all | solution.py:499
